TPU v7x, 256 devices: a whole 4x4x8 slice. The times are simulated.
256 devices in a mesh: region: 8 (over z), tile: 32 (over y, x, core).
Axes of the slice: x: 4, y: 4, z: 8, core: 2. Of those that a mesh axis runs over, the one named last changes fastest.
Arguments:
- offsets: float32 [2, 1048576], P(None, ('region', 'tile')), may hold values from 0 to 1
- design: float32 [2, 1048576], P(None, ('region', 'tile')), may hold values from -4 to 4
- target: float32 [1048576], P(('region', 'tile')), may hold values from -6 to 6
- beta_second: float32 [1048576], P(('region', 'tile')), may hold values from -3 to 3
- counts: int32 [4096], P(('region', 'tile')), may hold values from 1 to 256, as said below
- kernel_width: int32 [2, 4096], P(None, ('region', 'tile')), may hold values from 2 to 8
- reach: int32 [2, 4096, 9], P(None, ('region', 'tile')), may hold values 0 or 1
- assignment: int32 [8, 512], P('region', 'tile'), may hold values from 0 to 511, each once within a row
Outputs:
- betas: float32 [2, 1048576], P(None, ('region', 'tile'))
- hats: float32 [2, 1048576], P(None, ('region', 'tile'))
- residual: float32 [1048576], P(('region', 'tile'))
Inputs may be any that keep to these rules, and one draw needn't show every extreme that they name: `counts`: some tile holds 256 live records in every draw.
All inputs are finite; a program needn't handle non-finite values. No bound on the sum of `reach` on one device may be relied on, other than what follows from the above.
Results may differ from a plain program's by a relative error of at most 0.0003.
Values sent between devices are 32-bit elements; how exact they have to be, the bound alone decides.
A program may use at most 64 MiB of HBM per device.

v0:
```python
import jax
import jax.numpy as jnp
from jax import lax
from jax.sharding import PartitionSpec as P

TILE = 256
TX = 4


def with_halo(block, sides, width):
    for axis, dim in sides:
        count = lax.axis_size(axis)
        forward = [(i, i + 1) for i in range(count - 1)]
        backward = [(target, source) for source, target in forward]
        low = lax.ppermute(
            lax.slice_in_dim(block, block.shape[dim] - width, None, axis=dim), axis, forward
        )
        high = lax.ppermute(lax.slice_in_dim(block, 0, width, axis=dim), axis, backward)
        block = jnp.concatenate([low, block, high], axis=dim)
    return block


def spread_fields(fields, edge_plan):
    per_dev = fields.shape[1]
    tile_count = lax.axis_size("tile")
    strip_count = per_dev * tile_count
    padded_block = with_halo(fields, (("region", 1),), per_dev)
    received = lax.all_gather(padded_block, "tile", axis=1, tiled=True)
    side_of = jnp.arange(3 * strip_count, dtype=jnp.int32) // per_dev % 3 - 1
    return (received, edge_plan, side_of)


def smooth(
    own_east, own_north, own_cov, far_east, far_north, far_cov, far_part, valid, widths, present
):
    inverse_width = 32.0 / widths.astype(jnp.float32) ** 2
    weight_mask = jnp.repeat(valid, TILE, axis=1)
    squared = (own_east[:, :, None] - far_east[:, None, :]) ** 2 + (
        own_north[:, :, None] - far_north[:, None, :]
    ) ** 2
    kernel = jnp.exp(-squared * inverse_width[:, None, None]) * weight_mask[:, None, :]
    totals = 1.0 + jnp.einsum(
        "tij,tj->ti", kernel, far_cov * far_cov, precision=lax.Precision.HIGHEST
    )
    weighted = jnp.einsum("tij,tj->ti", kernel, far_cov * far_part, precision=lax.Precision.HIGHEST)
    return (present * weighted / totals, present * own_cov * own_cov / totals)


def body(offsets, design, target, beta_second, counts, kernel_width, reach, assignment):
    per_dev = counts.shape[0]
    strip_count = per_dev * lax.axis_size("tile")
    column_tiles = strip_count // TX
    region = lax.axis_index("region")
    geo_cell = assignment[0]
    column = geo_cell // column_tiles
    across = geo_cell % column_tiles
    places = offsets.reshape(2, per_dev, TILE)
    east_pos = (region * TX + column).astype(jnp.float32)[:, None] + places[0]
    north_pos = across.astype(jnp.float32)[:, None] + places[1]
    present = (jnp.arange(TILE, dtype=jnp.int32)[None, :] < counts[:, None]).astype(jnp.float32)
    cov_one = design[0].reshape(per_dev, TILE)
    cov_two = design[1].reshape(per_dev, TILE)
    observed = target.reshape(per_dev, TILE)
    prior_beta = beta_second.reshape(per_dev, TILE)
    partial_one = observed - cov_two * prior_beta
    geo_label = jnp.broadcast_to((geo_cell + 1).astype(jnp.float32)[:, None], (per_dev, TILE))
    fields = jnp.stack(
        [east_pos, north_pos, cov_one * present, cov_two * present, partial_one, geo_label]
    )
    received, edge_plan, side_of = spread_fields(fields, None)
    found_geo = received[5, :, 0].astype(jnp.int32)
    tile_keys = jnp.where(found_geo > 0, (side_of + 1) * strip_count + found_geo - 1, -1)
    step_cols = jnp.arange(9, dtype=jnp.int32) // 3 - 1
    step_rows = jnp.arange(9, dtype=jnp.int32) % 3 - 1
    near_cols = column[:, None] + step_cols[None, :]
    near_rows = across[:, None] + step_rows[None, :]
    side_near = jnp.where(near_cols < 0, -1, jnp.where(near_cols >= TX, 1, 0))
    wanted = (side_near + 1) * strip_count + (near_cols - side_near * TX) * column_tiles + near_rows
    inside = (near_rows >= 0) & (near_rows < column_tiles)
    matches = tile_keys[None, None, :] == wanted[:, :, None]
    located = jnp.any(matches, axis=2) & inside
    source = jnp.sum(
        jnp.where(matches, jnp.arange(tile_keys.shape[0], dtype=jnp.int32)[None, None, :], 0),
        axis=2,
    )
    flat_source = source.reshape(-1)
    nearby = jnp.take(received, flat_source, axis=1).reshape(6, per_dev, 9 * TILE)
    centre = (jnp.arange(9) == 4)[None, :]
    valid_one = (located & ((reach[0] > 0) | centre)).astype(jnp.float32)
    valid_two = (located & ((reach[1] > 0) | centre)).astype(jnp.float32)
    beta_one, hat_one = smooth(
        east_pos,
        north_pos,
        cov_one,
        nearby[0],
        nearby[1],
        nearby[2],
        nearby[4],
        valid_one,
        kernel_width[0],
        present,
    )
    partial_two = observed - cov_one * beta_one
    second_received, unused_plan, unused_sides = spread_fields(partial_two[None], edge_plan)
    far_partial = jnp.take(second_received[0], flat_source, axis=0).reshape(per_dev, 9 * TILE)
    beta_two, hat_two = smooth(
        east_pos,
        north_pos,
        cov_two,
        nearby[0],
        nearby[1],
        nearby[3],
        far_partial,
        valid_two,
        kernel_width[1],
        present,
    )
    residual = present * (observed - cov_one * beta_one - cov_two * beta_two)
    betas = jnp.stack([beta_one.reshape(-1), beta_two.reshape(-1)])
    hats = jnp.stack([hat_one.reshape(-1), hat_two.reshape(-1)])
    return (betas, hats, residual.reshape(-1))


def solution(mesh):
    in_specs = (
        P(None, ("region", "tile")),
        P(None, ("region", "tile")),
        P(("region", "tile")),
        P(("region", "tile")),
        P(("region", "tile")),
        P(None, ("region", "tile")),
        P(None, ("region", "tile"), None),
        P("region", "tile"),
    )
    out_specs = (P(None, ("region", "tile")), P(None, ("region", "tile")), P(("region", "tile")))
    return jax.shard_map(body, mesh=mesh, in_specs=in_specs, out_specs=out_specs, check_vma=False)
```

profile of v0, /device:TPU:1, one launch (start us, length us, event | category | flops | bytes accessed | tf_op | source)
XLA Modules:
  0.0 358.4 jit_solution(678902331210789843)
XLA Ops:
  7.2 0.0 all-gather.3.cloned.1.call-start
  7.2 1.0 slice_reduce_fusion.3
  8.3 0.7 reshape.487
  9.0 0.7 reshape.488
  9.8 0.7 add_convert_fusion
  10.4 0.1 add_dynamic-update-slice_fusion.1
  10.5 0.1 add_dynamic-update-slice_fusion
  10.6 0.7 select_dynamic-update-slice_fusion.1
  11.3 0.7 select_dynamic-update-slice_fusion
  12.0 0.1 constant_dynamic-update-slice_fusion
  12.1 4.4 %collective-permute-start = (f32[6,16,256]{2,1,0:T(8,128)S(1)}, f32[6,16,256]{2,1,0:T(8,128)S(1)}, u32[]{:S(2)}, u32[]{:S(2)}) collective-permute-start(f32[6,16,256]{2,1,0:T(8,128)S(1)} %constant_dynamic-update-slice_fusion), channel_id=1, source_target_pairs={{0,32},{32,64},{64,96},{96,128},{128,160},{160,192},{192,224},{1,3... | collective-permute-start | bytes 294920 | tf_op jit(solution)/shard_map/ppermute | solution.py:15
  16.5 1.3 collective-permute-start.1
  17.8 0.3 collective-permute-done
  18.1 3.9 %collective-permute-done.1 = f32[6,16,256]{2,1,0:T(8,128)S(1)} collective-permute-done((f32[6,16,256]{2,1,0:T(8,128)S(1)}, f32[6,16,256]{2,1,0:T(8,128)S(1)}, u32[]{:S(2)}, u32[]{:S(2)}) %collective-permute-start.1) | collective-permute-done | bytes 98336 | tf_op jit(solution)/shard_map/ppermute | solution.py:18
  22.0 0.7 pad_maximum_fusion
  22.7 0.0 all-gather.3.cloned.1.call-update
  22.8 0.0 all-gather.5.cloned.1.call-start
  22.8 0.7 reshape.491
  23.6 0.8 divide_bitcast_fusion.1
  24.4 0.1 add_add_fusion
  24.5 0.8 fusion.68
  25.2 0.1 broadcast_add_fusion
  25.3 0.1 broadcast_add_fusion.1
  25.4 62.2 %all-gather.3.cloned.1.call-done = f32[6,1536,256]{2,1,0:T(8,128)} async-done(((f32[6,48,256]{2,1,0:T(8,128)}), f32[6,1536,256]{2,1,0:T(8,128)}) %all-gather.3.cloned.1.call-update) | async-done | bytes 9437200 | tf_op jit(solution)/shard_map/all_gather | solution.py:28
  87.6 1.4 fusion.29
  89.1 0.3 fusion.28
  89.4 0.1 copy.22
  89.5 0.1 reshape.490
  89.6 0.1 reshape.489
  89.7 0.3 compare_reduce_fusion
  90.0 12.7 %copy.24 = f32[6,1536,256]{2,0,1:T(8,128)} copy(f32[6,1536,256]{2,1,0:T(8,128)} %all-gather.3.cloned.1.call-done) | data formatting | bytes 18874368 | tf_op jit(solution)/shard_map/all_gather | solution.py:28
  102.7 5.2 %gather_fusion = f32[144,6,256]{2,1,0:T(8,128)S(1)} fusion(f32[6,1536,256]{2,0,1:T(8,128)} %copy.24, s32[1024]{0:T(1024)S(1)} %pad_clamp_fusion), kind=kCustom, calls=%fused_computation | custom fusion | bytes 1770048 | tf_op jit(solution)/shard_map/jit(_take)/gather | solution.py:87
  108.0 0.2 select_bitcast_fusion
  108.2 1.4 slice_multiply_fusion
  109.7 0.1 fusion.53
  109.8 0.1 copy.26
  109.9 0.1 broadcast_in_dim.80
  110.0 0.1 copy.43
  110.1 44.8 %fusion.1 = f32[16,1,256]{2,1,0:T(1,128)S(1)} fusion(f32[16,2304,1]{1,2,0:T(1,128)S(1)} %bitcast.117, f32[16,2304]{1,0:T(8,128)S(1)} %bitcast.121, f32[16]{0:T(128)S(1)} %get-tuple-element.35, f32[16,2304]{1,0:T(8,128)S(1)} %sub.105, f32[16,256]{1,0:T(8,128)S(1)} %broadcast_add_fusion, f32[16,2304]{1,0:T(8,128)S(1)} %sub.101, ...), kind=kOutput, calls=%fused_computation.6 | convolution fusion | flops 188743680 | bytes 639040 | tf_op jit(solution)/shard_map/tij,tj->ti/dot_general | solution.py:45
  154.9 0.0 copy-start
  154.9 44.9 %fusion = f32[16,1,256]{2,1,0:T(1,128)S(1)} fusion(f32[16,2304,1]{1,2,0:T(1,128)S(1)} %bitcast.116, f32[16,2304]{1,0:T(8,128)S(1)} %bitcast.122, f32[16]{0:T(128)S(1)} %get-tuple-element.35, f32[16,2304]{1,0:T(8,128)S(1)} %sub.105, f32[16,256]{1,0:T(8,128)S(1)} %broadcast_add_fusion, f32[16,2304]{1,0:T(8,128)S(1)} %sub.101, ...), kind=kOutput, calls=%fused_computation.5 | convolution fusion | flops 188743680 | bytes 639040 | tf_op jit(solution)/shard_map/tij,tj->ti/dot_general | solution.py:42
  199.8 0.0 copy-done
  199.8 0.1 fusion.64
  199.9 3.2 collective-permute-start.2
  203.1 1.3 collective-permute-start.3
  204.4 0.0 collective-permute-done.2
  204.4 3.2 collective-permute-done.3
  207.6 0.6 pad_maximum_fusion.1
  208.2 0.0 all-gather.5.cloned.1.call-update
  208.3 0.1 copy.31
  208.4 0.1 broadcast_in_dim.82
  208.6 0.1 copy.30
  208.6 0.1 broadcast_in_dim.81
  208.7 0.1 copy.45
  208.9 48.7 %all-gather.5.cloned.1.call-done = f32[1,1536,256]{2,1,0:T(8,128)} async-done(((f32[1,48,256]{2,1,0:T(8,128)}), f32[1,1536,256]{2,1,0:T(8,128)}) %all-gather.5.cloned.1.call-update) | async-done | bytes 1572880 | tf_op jit(solution)/shard_map/all_gather | solution.py:28
  257.6 2.2 gather_fusion.1
  259.9 44.8 %fusion.3 = f32[16,1,256]{2,1,0:T(1,128)S(1)} fusion(f32[16,2304]{1,0:T(8,128)S(1)} %bitcast.119, f32[16]{0:T(128)S(1)} %get-tuple-element.36, f32[16,2304]{1,0:T(8,128)S(1)} %sub.105, f32[16,256]{1,0:T(8,128)S(1)} %broadcast_add_fusion, f32[16,2304]{1,0:T(8,128)S(1)} %sub.101, f32[16,256]{1,0:T(8,128)S(1)} %broadcast_add_fusion.1, ...), kind=kOutput, calls=%fused_computation.8 | convolution fusion | flops 188743680 | bytes 639040 | tf_op jit(solution)/shard_map/tij,tj->ti/dot_general | solution.py:45
  304.7 44.8 %fusion.2 = f32[16,1,256]{2,1,0:T(1,128)S(1)} fusion(f32[16,2304]{1,0:T(8,128)S(1)} %bitcast.120, f32[16]{0:T(128)S(1)} %get-tuple-element.36, f32[16,2304]{1,0:T(8,128)S(1)} %sub.105, f32[16,256]{1,0:T(8,128)S(1)} %broadcast_add_fusion, f32[16,2304]{1,0:T(8,128)S(1)} %sub.101, f32[16,256]{1,0:T(8,128)S(1)} %broadcast_add_fusion.1, ...), kind=kOutput, calls=%fused_computation.7 | convolution fusion | flops 188743680 | bytes 639040 | tf_op jit(solution)/shard_map/tij,tj->ti/dot_general | solution.py:42
  349.5 0.1 select_bitcast_fusion.1
  349.6 0.6 copy.50
  350.2 0.6 pad_maximum_fusion.3
  350.9 0.6 pad_maximum_fusion.2
  (26 shorter events, 0.4 us)
Async XLA Ops:
  7.2 80.5 %all-gather.3.cloned.1.call-start = ((), (), s32[]{:S(2)}) async-start(), calls=%async_computation | async-start | bytes 9732096 | tf_op jit(solution)/shard_map/all_gather | solution.py:28
  12.1 6.0 %collective-permute-start = (f32[6,16,256]{2,1,0:T(8,128)S(1)}, f32[6,16,256]{2,1,0:T(8,128)S(1)}, u32[]{:S(2)}, u32[]{:S(2)}) collective-permute-start(f32[6,16,256]{2,1,0:T(8,128)S(1)} %constant_dynamic-update-slice_fusion), channel_id=1, source_target_pairs={{0,32},{32,64},{64,96},{96,128},{128,160},{160,192},{192,224},{1,3... | collective-permute-start | bytes 294920 | tf_op jit(solution)/shard_map/ppermute | solution.py:15
  16.5 5.5 %collective-permute-start.1 = (f32[6,16,256]{2,1,0:T(8,128)S(1)}, f32[6,16,256]{2,1,0:T(8,128)S(1)}, u32[]{:S(2)}, u32[]{:S(2)}) collective-permute-start(f32[6,16,256]{2,1,0:T(8,128)S(1)} %constant_dynamic-update-slice_fusion), channel_id=1, source_target_pairs={{32,0},{64,32},{96,64},{128,96},{160,128},{192,160},{224,192},{33,... | collective-permute-start | bytes 294920 | tf_op jit(solution)/shard_map/ppermute | solution.py:18
  22.8 234.8 %all-gather.5.cloned.1.call-start = ((), (), s32[]{:S(2)}) async-start(), calls=%async_computation.1 | async-start | bytes 1622016 | tf_op jit(solution)/shard_map/all_gather | solution.py:28
  154.9 44.9 %copy-start = (s32[16]{0:T(128)S(1)}, s32[16]{0:T(128)}, u32[]{:S(2)}) copy-start(s32[16]{0:T(128)} %param.12) | copy-start | bytes 196
  199.9 4.5 %collective-permute-start.2 = (f32[1,16,256]{2,1,0:T(8,128)S(1)}, f32[1,16,256]{2,1,0:T(8,128)S(1)}, u32[]{:S(2)}, u32[]{:S(2)}) collective-permute-start(f32[1,16,256]{2,1,0:T(8,128)S(1)} %get-tuple-element.10), channel_id=1, source_target_pairs={{0,32},{32,64},{64,96},{96,128},{128,160},{160,192},{192,224},{1,3... | collective-permute-start | bytes 49160 | tf_op jit(solution)/shard_map/ppermute | solution.py:15
  203.1 4.5 %collective-permute-start.3 = (f32[1,16,256]{2,1,0:T(8,128)S(1)}, f32[1,16,256]{2,1,0:T(8,128)S(1)}, u32[]{:S(2)}, u32[]{:S(2)}) collective-permute-start(f32[1,16,256]{2,1,0:T(8,128)S(1)} %get-tuple-element.10), channel_id=1, source_target_pairs={{32,0},{64,32},{96,64},{128,96},{160,128},{192,160},{224,192},{33,... | collective-permute-start | bytes 49160 | tf_op jit(solution)/shard_map/ppermute | solution.py:18
Sparse Core Ops, SparseCore 0:
  22.9 64.6 all-gather.2
  208.4 49.1 all-gather.4
where the time goes:
time: 359 us; the launch traced here: 358 us
  matrix products  179 us (50%)
  waiting for transfers between devices  118 us (33%)
  local copies, waits for them, and re-layouts  26.1 us (7%)
  between operations  14.4 us (4%)
  starting transfers between devices  10.2 us (3%)
  other arithmetic  9.99 us (3%)
    all_gather x2, waiting for transfers between devices, spread_fields(): received = lax.all_gather(padded_block, 'tile', axis=1, tiled=True)  111 us
    dot_general x2, matrix products, smooth(): jnp.einsum('tij,tj->ti', kernel, far_cov * far_cov, precision=lax.Precisi...  89.7 us
    dot_general x2, matrix products, smooth(): jnp.einsum('tij,tj->ti', kernel, far_cov * far_part, precision=lax.Precis...  89.6 us
    all_gather x1, local copies, waits for them, and re-layouts, spread_fields(): received = lax.all_gather(padded_block, 'tile', axis=1, tiled=True)  12.7 us
    ppermute x2, starting transfers between devices, with_halo(): lax.ppermute(lax.slice_in_dim(block, block.shape[dim] - width, None, axis...  7.53 us
  transfers between devices with their start and end apart: 6, of which 5 were waited for; matrix products, arithmetic and copies ran while one was open for 1% of the time, Pallas kernels for 0%

commit v1 on v0

v1 whole, which is shorter than its diff:
```python
import functools
import math

import jax
import jax.numpy as jnp
from jax import lax
from jax.experimental import pallas as pl
from jax.experimental.pallas import tpu as pltpu
from jax.sharding import PartitionSpec as P

TX = 4
LANES = 128
PER = 16
NPIECE = 13
KDIM = 32
NREGION = 8
NTILE = 32
F32 = jnp.float32
BF16 = jnp.bfloat16


def split3(x):
    hi = x.astype(BF16).astype(F32)
    rest = x - hi
    mid = rest.astype(BF16).astype(F32)
    low = (rest - mid).astype(BF16).astype(F32)
    return hi, mid, low


def wide_split(x):
    hi, mid, low = split3(x)
    return jnp.concatenate([hi.astype(BF16), mid.astype(BF16), low.astype(BF16)], axis=1)


def join3(x):
    return x[:, :LANES] + x[:, LANES : 2 * LANES] + x[:, 2 * LANES :]


def remote(src, dst, send, recv, region, tile):
    return pltpu.make_async_remote_copy(
        src_ref=src,
        dst_ref=dst,
        send_sem=send,
        recv_sem=recv,
        device_id=(region, tile),
        device_id_type=pl.DeviceIdType.MESH,
    )


def signal(sem, region, tile):
    pl.semaphore_signal(sem, inc=1, device_id=(region, tile), device_id_type=pl.DeviceIdType.MESH)


def each(low, high, step):
    def turn(index, carry):
        step(index)
        return carry

    lax.fori_loop(low, high, turn, 0)


def gather_kernel(
    offs, design, target, prior, meta, data_out, meta_out, cells_out,
    stage, rbuf, msg, recv, send1, recv1, send2, recv2,
):
    region = lax.axis_index("region")
    tile = lax.axis_index("tile")
    group = tile // 16
    piece = lax.rem(tile, 16)
    up = lax.rem(region + 1, NREGION)
    down = lax.rem(region + NREGION - 1, NREGION)

    barrier = pltpu.get_barrier_semaphore()
    each(1, NTILE, lambda o: signal(barrier, region, lax.rem(tile + o, NTILE)))
    each(0, 16, lambda i: signal(barrier, up, group * 16 + i))
    each(0, 16, lambda i: signal(barrier, down, group * 16 + i))

    lane = lax.broadcasted_iota(jnp.int32, (PER, LANES), 1)
    count = meta[0:PER, 0:1]
    for h in range(2):
        present = ((lane + LANES * h).astype(F32) < count).astype(F32)
        east = offs[pl.ds(2 * h, PER, stride=4), :]
        north = offs[pl.ds(2 * h + 1, PER, stride=4), :]
        cov_one = design[pl.ds(2 * h, PER, stride=4), :]
        cov_two = design[pl.ds(2 * h + 1, PER, stride=4), :]
        seen = target[pl.ds(h, PER, stride=2), :]
        before = prior[pl.ds(h, PER, stride=2), :]
        values = (
            east, north, cov_one * present, seen - cov_two * before, cov_two * present, seen,
        )
        for f, value in enumerate(values):
            stage[2 * f + h, 0:PER, :] = value
    stage[12, 0:PER, :] = meta[0:PER, :]
    row_lane = lax.broadcasted_iota(jnp.int32, (8, LANES), 1)
    cell_row = jnp.where(row_lane // PER == lax.rem(tile, 8), meta[PER : PER + 8, :], 0.0)
    for p in range(NPIECE):
        stage[p, PER : PER + 8, :] = cell_row

    pl.semaphore_wait(barrier, NTILE - 1 + 32)

    def to_middle(o):
        other = lax.rem(tile + o, NTILE)
        held = jnp.minimum(lax.rem(other, 16), NPIECE - 1)
        return remote(
            stage.at[held, pl.ds(0, PER + 1)], rbuf.at[tile, pl.ds(0, PER + 1)],
            send1.at[o], recv1.at[tile], region, other,
        )

    each(1, NTILE, lambda o: to_middle(o).start())
    rbuf[tile] = stage[jnp.minimum(piece, NPIECE - 1)]

    def from_source(o):
        other = lax.rem(tile + o, NTILE)
        return remote(
            stage.at[0, pl.ds(0, PER + 1)], rbuf.at[other, pl.ds(0, PER + 1)],
            send1.at[o], recv1.at[other], region, other,
        )

    each(1, NTILE, lambda o: from_source(o).wait_recv())

    cell_rows = [
        jnp.sum(rbuf[8 * b : 8 * b + 8, PER, :], axis=0, keepdims=True) for b in range(4)
    ]
    for b in range(4):
        cells_out[b : b + 1, :] = cell_rows[b]
    cells_out[4:8, :] = jnp.zeros((4, LANES), F32)

    @pl.when(piece < NPIECE)
    def _():
        spread = wide_split(rbuf[:, 0:PER, :].reshape(NTILE * PER, LANES))
        number = lax.broadcasted_iota(jnp.int32, (640, LANES), 0)
        owner = lax.shift_right_logical(number * 205, 13)
        q = number - owner * 40
        first = (group * 16 + owner) * 16
        side = jnp.where(q < 32, q - 24, q - 32)
        base = jnp.where(q < 24, q - 4, (side - 1) * 4 + jnp.where(q < 32, 3, 0))
        open_up = jnp.where(region < NREGION - 1, 1, 0)
        open_down = jnp.where(region > 0, 1, 0)
        beside = jnp.where(side < 6, jnp.where(q < 32, open_up, open_down), 0)
        allowed = jnp.where(q < 24, 1, beside)
        cell = first + base
        wanted = jnp.where(allowed > 0, cell, -1).astype(F32)
        hot = jnp.concatenate(
            [jnp.where(wanted == cell_rows[b], 1.0, 0.0).astype(BF16) for b in range(4)], axis=1
        )
        moved = join3(jnp.dot(hot, spread, preferred_element_type=F32))
        msg[...] = moved.reshape(16, 40, LANES)

    def own_copy(o):
        i = lax.rem(piece + o, 16)
        return remote(
            msg.at[i, pl.ds(0, 24)], recv.at[piece, pl.ds(0, 24)],
            send2.at[0, o], recv2.at[0, piece], region, group * 16 + i,
        )

    def up_copy(i):
        return remote(
            msg.at[i, pl.ds(24, 8)], recv.at[piece, pl.ds(24, 8)],
            send2.at[1, i], recv2.at[1, piece], up, group * 16 + i,
        )

    def down_copy(i):
        return remote(
            msg.at[i, pl.ds(32, 8)], recv.at[piece, pl.ds(32, 8)],
            send2.at[2, i], recv2.at[2, piece], down, group * 16 + i,
        )

    @pl.when(piece < NPIECE)
    def _():
        each(1, 16, lambda o: own_copy(o).start())
        each(0, 16, lambda i: up_copy(i).start())
        each(0, 16, lambda i: down_copy(i).start())
        recv[piece, 0:24, :] = msg[piece, 0:24, :]

    def wait_own(p):
        @pl.when(p != piece)
        def _():
            remote(
                msg.at[0, pl.ds(0, 24)], recv.at[p, pl.ds(0, 24)],
                send2.at[0, 0], recv2.at[0, p], region, group * 16 + p,
            ).wait_recv()

    def wait_sides(p):
        remote(
            msg.at[0, pl.ds(24, 8)], recv.at[p, pl.ds(24, 8)],
            send2.at[1, 0], recv2.at[1, p], down, group * 16 + p,
        ).wait_recv()
        remote(
            msg.at[0, pl.ds(32, 8)], recv.at[p, pl.ds(32, 8)],
            send2.at[2, 0], recv2.at[2, p], up, group * 16 + p,
        ).wait_recv()

    each(0, NPIECE, wait_own)
    each(0, NPIECE, wait_sides)
    for p in range(12):
        data_out[p] = recv[p]
    meta_out[...] = recv[12].astype(jnp.int32)

    each(1, NTILE, lambda o: to_middle(o).wait_send())

    @pl.when(piece < NPIECE)
    def _():
        each(1, 16, lambda o: own_copy(o).wait_send())
        each(0, 16, lambda i: up_copy(i).wait_send())
        each(0, 16, lambda i: down_copy(i).wait_send())


def smooth_kernel(which, data, meta, counts, *refs):
    if which == 0:
        beta_out, hat_out, pull_out, left, right, cross, square, pull, turned = refs
    else:
        grid, beta_out, hat_out, left, right, cross, square, pull, turned = refs
    slot = lax.broadcasted_iota(jnp.int32, (40, LANES), 0)
    col = jnp.where(slot < 24, lax.rem(slot, 4) + 1, jnp.where(slot < 32, 0, 5))
    row = jnp.where(slot < 24, slot // 4, jnp.where(slot < 32, slot - 24, slot - 32))
    col = col.astype(F32) - 3.0
    row = row.astype(F32) - 3.0
    width = meta[4:20, 1 + which : 2 + which].astype(F32)
    rate = jnp.broadcast_to((32.0 * math.log2(math.e)) / (width * width), (PER, LANES))
    rates = split3(rate)
    pairs = ((0, 0), (0, 1), (1, 0), (1, 1), (0, 2), (2, 0))
    zero40 = jnp.zeros((40, LANES), F32)
    zero16 = jnp.zeros((PER, LANES), F32)
    for h in range(2):
        x = data[h] + col
        y = data[2 + h] + row
        far = -(x * x + y * y)
        own_x, own_y, own_far = x[4:20], y[4:20], far[4:20]
        lefts = (split3(2.0 * rate * own_x), split3(2.0 * rate * own_y), rates)
        rights = (split3(x), split3(y), split3(far))
        k = 0
        for one, two in zip(lefts, rights):
            for a, b in pairs:
                left[h, pl.ds(k, PER, stride=KDIM), :] = one[a]
                cross[h, pl.ds(k, 40, stride=KDIM), :] = two[b]
                k += 1
        for part in split3(rate * own_far):
            left[h, pl.ds(k, PER, stride=KDIM), :] = part
            cross[h, pl.ds(k, 40, stride=KDIM), :] = zero40 + 1.0
            k += 1
        while k < KDIM:
            left[h, pl.ds(k, PER, stride=KDIM), :] = zero16
            cross[h, pl.ds(k, 40, stride=KDIM), :] = zero40
            k += 1
        cov = data[4 + 4 * which + h]
        square[h] = cov * cov
        if which == 0:
            pull[h] = cov * data[6 + h]
        else:
            pull[h] = grid[h]

    def pack(t):
        for h in range(2):
            right[h, t] = cross[h, pl.ds(pl.multiple_of(t * KDIM, KDIM), KDIM), :].astype(BF16)

    each(0, 40, pack)

    def turn(i):
        for h in range(2):
            rows = left[h, pl.ds(pl.multiple_of(i * KDIM, KDIM), KDIM), :]
            turned[h, i] = jnp.transpose(rows).astype(BF16)

    each(0, PER, turn)

    ones = jnp.ones((8, LANES), F32)
    sums = functools.partial(
        lax.dot_general, dimension_numbers=(((1,), (1,)), ((), ())),
        precision=lax.Precision.HIGHEST, preferred_element_type=F32,
    )
    lane = lax.broadcasted_iota(jnp.int32, (1, LANES), 1)

    def one_tile(i):
        down = i // 4 + 1
        over = lax.rem(i, 4) + 1
        places, keeps = [], []
        for e in range(9):
            c = over + (e // 3 - 1)
            r = down + (e % 3 - 1)
            places.append(jnp.where(c == 0, 24 + r, jnp.where(c == 5, 32 + r, r * 4 + c - 1)))
            if e == 4:
                keeps.append(None)
            else:
                keeps.append(jnp.where(counts[4 + i, 3 + 9 * which + e] > 0, 1.0, 0.0))
        count = counts[4 + i, 0]
        for h in range(2):
            points = turned[h, i]
            weight_sum = jnp.zeros((LANES, LANES), F32)
            pull_sum = jnp.zeros((LANES, LANES), F32)
            for e in range(9):
                t = places[e]
                for g in range(2):
                    weight = jnp.exp2(jnp.dot(points, right[g, t], preferred_element_type=F32))
                    heavy = square[g, pl.ds(t, 1), :]
                    drawn = pull[g, pl.ds(t, 1), :]
                    if keeps[e] is not None:
                        heavy = heavy * keeps[e]
                        drawn = drawn * keeps[e]
                    weight_sum += weight * heavy
                    pull_sum += weight * drawn
            total = 1.0 + sums(ones, weight_sum)[0:1]
            drawn = sums(ones, pull_sum)[0:1]
            live = (lane + LANES * h < count).astype(F32)
            beta = live * drawn / total
            beta_out[h, pl.ds(i, 1), :] = beta
            hat_out[h, pl.ds(i, 1), :] = live * square[h, pl.ds(4 + i, 1), :] / total
            if which == 0:
                seen = data[10 + h, pl.ds(4 + i, 1), :]
                cov_one = data[4 + h, pl.ds(4 + i, 1), :]
                cov_two = data[8 + h, pl.ds(4 + i, 1), :]
                pull_out[h, pl.ds(i, 1), :] = cov_two * (seen - cov_one * beta)

    each(0, PER, one_tile)


def halo_kernel(own, grid_out, recv, send, land):
    region = lax.axis_index("region")
    tile = lax.axis_index("tile")
    steps = [(a, b) for a in (-1, 0, 1) for b in (-1, 0, 1) if (a, b) != (0, 0)]

    def place(a, b):
        return lax.rem(region + a + NREGION, NREGION), lax.rem(tile + b + NTILE, NTILE)

    barrier = pltpu.get_barrier_semaphore()
    for a, b in steps:
        signal(barrier, *place(a, b))
    pl.semaphore_wait(barrier, 8)
    copies = []
    for k, (a, b) in enumerate(steps):
        copies.append(remote(own, recv.at[7 - k], send.at[k], land.at[7 - k], *place(a, b)))
    for copy in copies:
        copy.start()
    for copy in copies:
        copy.wait_recv()
    fits = {-1: region > 0, 0: None, 1: region < NREGION - 1}
    fits_row = {-1: tile > 0, 0: None, 1: tile < NTILE - 1}
    at = {step: k for k, step in enumerate(steps)}

    def take(h, a, b, low, high):
        rows = recv[at[(a, b)], h, low:high, :]
        for fit in (fits[a], fits_row[b]):
            if fit is not None:
                rows = jnp.where(fit, rows, 0.0)
        return rows

    for h in range(2):
        grid_out[h, 4:20, :] = own[h]
        grid_out[h, 0:4, :] = take(h, 0, -1, 12, 16)
        grid_out[h, 20:24, :] = take(h, 0, 1, 0, 4)
        for a, edge, first in ((-1, 3, 24), (1, 0, 32)):
            grid_out[h, first : first + 1, :] = take(h, a, -1, 12 + edge, 13 + edge)
            for r in range(4):
                grid_out[h, first + 1 + r : first + 2 + r, :] = take(h, a, 0, 4 * r + edge, 4 * r + edge + 1)
            grid_out[h, first + 5 : first + 6, :] = take(h, a, 1, edge, edge + 1)
            grid_out[h, first + 6 : first + 8, :] = jnp.zeros((2, LANES), F32)
    for copy in copies:
        copy.wait_send()


def return_kernel(
    beta_one, hat_one, beta_two, hat_two, cells, design, target, meta, betas, hats, residual,
    stage, rbuf, msg, recv, send1, recv1, send2, recv2,
):
    region = lax.axis_index("region")
    tile = lax.axis_index("tile")
    group = tile // 8
    piece = lax.rem(tile, 8)
    barrier = pltpu.get_barrier_semaphore()
    each(1, NTILE, lambda o: signal(barrier, region, lax.rem(tile + o, NTILE)))
    for f, ref in enumerate((beta_one, hat_one, beta_two, hat_two)):
        for h in range(2):
            stage[2 * f + h] = ref[h]
    pl.semaphore_wait(barrier, NTILE - 1)

    def to_middle(o):
        other = lax.rem(tile + o, NTILE)
        return remote(
            stage.at[lax.rem(other, 8)], rbuf.at[tile], send1.at[o], recv1.at[tile], region, other
        )

    each(1, NTILE, lambda o: to_middle(o).start())
    rbuf[tile] = stage[piece]

    row = cells[pl.ds(group, 1), :]
    column = jnp.transpose(jnp.broadcast_to(row, (LANES, LANES)))
    lane = lax.broadcasted_iota(jnp.int32, (LANES, LANES), 1)
    hot = jnp.concatenate(
        [
            jnp.where((lane + LANES * b).astype(F32) == column, 1.0, 0.0).astype(BF16)
            for b in range(4)
        ],
        axis=1,
    )

    def from_source(o):
        other = lax.rem(tile + o, NTILE)
        return remote(stage.at[0], rbuf.at[other], send1.at[o], recv1.at[other], region, other)

    each(1, NTILE, lambda o: from_source(o).wait_recv())
    spread = wide_split(rbuf[...].reshape(NTILE * PER, LANES))
    msg[...] = join3(jnp.dot(hot, spread, preferred_element_type=F32)).reshape(8, PER, LANES)

    def home_copy(o):
        i = lax.rem(piece + o, 8)
        return remote(
            msg.at[i], recv.at[piece], send2.at[o], recv2.at[piece], region, group * 8 + i
        )

    each(1, 8, lambda o: home_copy(o).start())
    recv[piece] = msg[piece]

    def from_middle(o):
        p = lax.rem(piece + o, 8)
        return remote(msg.at[0], recv.at[p], send2.at[o], recv2.at[p], region, group * 8 + p)

    each(1, 8, lambda o: from_middle(o).wait_recv())
    wide = lax.broadcasted_iota(jnp.int32, (PER, LANES), 1)
    count = meta[0:PER, 0:1]
    for h in range(2):
        present = ((wide + LANES * h).astype(F32) < count).astype(F32)
        one, two = recv[h], recv[4 + h]
        cov_one = design[pl.ds(2 * h, PER, stride=4), :]
        cov_two = design[pl.ds(2 * h + 1, PER, stride=4), :]
        seen = target[pl.ds(h, PER, stride=2), :]
        betas[pl.ds(2 * h, PER, stride=4), :] = one
        betas[pl.ds(2 * h + 1, PER, stride=4), :] = two
        hats[pl.ds(2 * h, PER, stride=4), :] = recv[2 + h]
        hats[pl.ds(2 * h + 1, PER, stride=4), :] = recv[6 + h]
        residual[pl.ds(h, PER, stride=2), :] = present * (seen - cov_one * one - cov_two * two)
    each(1, NTILE, lambda o: to_middle(o).wait_send())
    each(1, 8, lambda o: home_copy(o).wait_send())


VM = pl.BlockSpec(memory_space=pltpu.VMEM)
SM = pl.BlockSpec(memory_space=pltpu.SMEM)
DMA = pltpu.SemaphoreType.DMA


def shape(*dims, dtype=F32):
    return jax.ShapeDtypeStruct(dims, dtype)


def smooth(which, data, meta, *extra):
    outs = [shape(2, PER, LANES)] * (3 if which == 0 else 2)
    return pl.pallas_call(
        functools.partial(smooth_kernel, which),
        out_shape=outs,
        in_specs=[VM, VM, SM] + [VM] * len(extra),
        out_specs=[VM] * len(outs),
        scratch_shapes=[
            pltpu.VMEM((2, PER * KDIM, LANES), F32),
            pltpu.VMEM((2, 40, KDIM, LANES), BF16),
            pltpu.VMEM((2, 40 * KDIM, LANES), F32),
            pltpu.VMEM((2, 40, LANES), F32),
            pltpu.VMEM((2, 40, LANES), F32),
            pltpu.VMEM((2, PER, LANES, KDIM), BF16),
        ],
        name="smooth_one" if which == 0 else "smooth_two",
    )(data, meta, meta, *extra)


def body(offsets, design, target, beta_second, counts, kernel_width, reach, assignment):
    def rows(pair):
        return pair.reshape(2, NTILE, LANES).transpose(1, 0, 2).reshape(2 * NTILE, LANES)

    offs, design = rows(offsets), rows(design)
    target = target.reshape(NTILE, LANES)
    prior = beta_second.reshape(NTILE, LANES)
    cell = assignment[0]
    order = (cell % 128) * TX + cell // 128
    notes = jnp.concatenate([counts[:, None], kernel_width.T, reach[0], reach[1]], axis=1)
    meta = jnp.concatenate(
        [
            jnp.pad(notes, ((0, 0), (0, LANES - 21))),
            jnp.broadcast_to(jnp.tile(order, 8)[None], (8, LANES)),
        ],
        axis=0,
    ).astype(F32)
    data, own_meta, cells = pl.pallas_call(
        gather_kernel,
        out_shape=[shape(12, 40, LANES), shape(40, LANES, dtype=jnp.int32), shape(8, LANES)],
        in_specs=[VM] * 5,
        out_specs=[VM] * 3,
        scratch_shapes=[
            pltpu.VMEM((NPIECE, 24, LANES), F32),
            pltpu.VMEM((NTILE, 24, LANES), F32),
            pltpu.VMEM((16, 40, LANES), F32),
            pltpu.VMEM((NPIECE, 40, LANES), F32),
            DMA((NTILE,)),
            DMA((NTILE,)),
            DMA((3, 16)),
            DMA((3, 16)),
        ],
        compiler_params=pltpu.CompilerParams(collective_id=0, has_side_effects=True),
        name="to_owners",
    )(offs, design, target, prior, meta)
    beta_one, hat_one, pull = smooth(0, data, own_meta)
    grid = pl.pallas_call(
        halo_kernel,
        out_shape=shape(2, 40, LANES),
        in_specs=[VM],
        out_specs=VM,
        scratch_shapes=[pltpu.VMEM((8, 2, PER, LANES), F32), DMA((8,)), DMA((8,))],
        compiler_params=pltpu.CompilerParams(collective_id=1, has_side_effects=True),
        name="edges",
    )(pull)
    beta_two, hat_two = smooth(1, data, own_meta, grid)
    betas, hats, residual = pl.pallas_call(
        return_kernel,
        out_shape=[shape(64, LANES), shape(64, LANES), shape(NTILE, LANES)],
        in_specs=[VM] * 8,
        out_specs=[VM] * 3,
        scratch_shapes=[
            pltpu.VMEM((8, PER, LANES), F32),
            pltpu.VMEM((NTILE, PER, LANES), F32),
            pltpu.VMEM((8, PER, LANES), F32),
            pltpu.VMEM((8, PER, LANES), F32),
            DMA((NTILE,)),
            DMA((NTILE,)),
            DMA((8,)),
            DMA((8,)),
        ],
        compiler_params=pltpu.CompilerParams(collective_id=2, has_side_effects=True),
        name="to_slots",
    )(beta_one, hat_one, beta_two, hat_two, cells, design, target, meta)

    def flat(pair):
        return pair.reshape(NTILE, 2, LANES).transpose(1, 0, 2).reshape(2, NTILE * LANES)

    return flat(betas), flat(hats), residual.reshape(-1)


def solution(mesh):
    split = ("region", "tile")
    in_specs = (
        P(None, split), P(None, split), P(split), P(split), P(split), P(None, split),
        P(None, split, None), P("region", "tile"),
    )
    out_specs = (P(None, split), P(None, split), P(split))
    return jax.shard_map(body, mesh=mesh, in_specs=in_specs, out_specs=out_specs, check_vma=False)
```

time: 359 us -> 114 us (0.32)
  matrix products: 179 us -> 0 us
  waiting for transfers between devices: 118 us -> 0 us
  Pallas kernels: 0 us -> 107 us
  local copies, waits for them, and re-layouts: 26.1 us -> 4.97 us
  between operations: 14.4 us -> 0.7 us
  starting transfers between devices: 10.2 us -> 0 us
  other arithmetic: 9.99 us -> 0.7 us
    dot_general x4 -> x0, matrix products: 179 us -> none  [the longest x2 89.7 us: smooth(): jnp.einsum('tij,tj->ti', kernel, far_cov * far_cov, precision=lax.Precisi...]
    all_gather x2 -> x0, waiting for transfers between devices: 111 us -> none  [spread_fields(): received = lax.all_gather(padded_block, 'tile', axis=1, tiled=True)]
    pallas_call x0 -> x5, Pallas kernels: none -> 107 us  [the longest x2 54.1 us: smooth(): pl.pallas_call(functools.partial(smooth_kernel, which), out_shape=outs, i...]
    all_gather x1 -> x0, local copies, waits for them, and re-layouts: 12.7 us -> none  [spread_fields(): received = lax.all_gather(padded_block, 'tile', axis=1, tiled=True)]
    ppermute x4 -> x0, starting transfers between devices: 10.1 us -> none  [the longest x2 7.53 us: with_halo(): lax.ppermute(lax.slice_in_dim(block, block.shape[dim] - width, None, axis...]
    gather x3 -> x0, local copies, waits for them, and re-layouts: 7.47 us -> none  [the longest x1 5.24 us: body(): jnp.take(received, flat_source, axis=1).reshape(6, per_dev, 9 * TILE)]
    ppermute x4 -> x0, waiting for transfers between devices: 7.42 us -> none  [the longest x2 7.1 us: with_halo(): lax.ppermute(lax.slice_in_dim(block, 0, width, axis=dim), axis, backward)]
    unnamed x10 -> x18, local copies, waits for them, and re-layouts: 0.9 us -> 4.79 us
  transfers between devices with their start and end apart: 6 -> 0, of which waited for: 5 -> 0; matrix products, arithmetic and copies ran while one was open for 1% -> 0% of each run, Pallas kernels for 0% -> 0%
where the time goes in v1:
time: 114 us
  Pallas kernels  107 us (94%)
  local copies, waits for them, and re-layouts  4.97 us (4%)
    pallas_call x2, Pallas kernels, smooth(): pl.pallas_call(functools.partial(smooth_kernel, which), out_shape=outs, i...  54.1 us
    pallas_call x1, Pallas kernels, body(): pl.pallas_call(gather_kernel, out_shape=[shape(12, 40, LANES), shape(40,...  28 us
    pallas_call x1, Pallas kernels, body(): pl.pallas_call(return_kernel, out_shape=[shape(64, LANES), shape(64, LANE...  18.3 us
    pallas_call x1, Pallas kernels, body(): pl.pallas_call(halo_kernel, out_shape=shape(2, 40, LANES), in_specs=[VM],...  6.94 us
    unnamed x18, local copies, waits for them, and re-layouts  4.79 us

profile of v1, /device:TPU:1, one launch (start us, length us, event | category | flops | bytes accessed | tf_op | source)
XLA Modules:
  0.0 113.7 jit_solution(6117795526474491950)
XLA Ops:
  0.6 0.0 copy-start.5
  0.6 0.6 copy-done.5
  1.3 0.1 broadcast_in_dim.11
  1.4 0.0 copy-start.4
  1.4 0.0 copy-start.3
  1.4 0.6 copy-done.4
  2.0 0.0 copy-start.2
  2.1 0.1 copy.16
  2.1 0.0 copy-done.3
  2.1 0.1 copy.13
  2.2 0.5 copy-done.2
  2.8 0.1 copy.19
  2.8 0.1 copy.20
  2.9 0.1 pad_add_fusion.1
  3.0 0.6 fusion.meta
  3.6 28.0 %to_owners.1 = (f32[12,40,128]{2,1,0:T(8,128)}, s32[40,128]{1,0:T(8,128)}, f32[8,128]{1,0:T(8,128)}) custom-call(f32[64,128]{1,0:T(8,128)} %bitcast.33, f32[64,128]{1,0:T(8,128)} %bitcast.29, f32[32,128]{1,0:T(8,128)} %bitcast.31, f32[32,128]{1,0:T(8,128)} %bitcast.39, f32[24,128]{1,0:T(8,128)} %fusion.meta), custom_call_target="tpu_custom_call" | custom-call | tf_op jit(solution)/shard_map/to_owners/pallas_call | solution.py:478
  31.7 27.1 %smooth_one.1 = (f32[2,16,128]{2,1,0:T(8,128)}, f32[2,16,128]{2,1,0:T(8,128)}, f32[2,16,128]{2,1,0:T(8,128)}) custom-call(f32[12,40,128]{2,1,0:T(8,128)} %get-tuple-element.14.data, s32[40,128]{1,0:T(8,128)} %get-tuple-element.15.meta.counts, s32[40,128]{1,0:T(8,128)} %get-tuple-element.15.meta.counts), custom_call_target="tpu_custom_call" | custom-call | tf_op jit(solution)/shard_map/smooth_one/pallas_call | solution.py:444
  58.7 6.9 %edges.1.refs_0_ = f32[2,40,128]{2,1,0:T(8,128)} custom-call(f32[2,16,128]{2,1,0:T(8,128)} %get-tuple-element.18.own), custom_call_target="tpu_custom_call" | custom-call | tf_op jit(solution)/shard_map/edges/pallas_call | solution.py:497
  65.7 27.0 %smooth_two.1 = (f32[2,16,128]{2,1,0:T(8,128)}, f32[2,16,128]{2,1,0:T(8,128)}) custom-call(f32[12,40,128]{2,1,0:T(8,128)} %get-tuple-element.14.data, s32[40,128]{1,0:T(8,128)} %get-tuple-element.15.meta.counts, s32[40,128]{1,0:T(8,128)} %get-tuple-element.15.meta.counts, f32[2,40,128]{2,1,0:T(8,128)} %edges.1.refs_0_), custom_call_target="tpu_custom_call" | custom-call | tf_op jit(solution)/shard_map/smooth_two/pallas_call | solution.py:444
  92.7 18.3 %to_slots.1 = (f32[64,128]{1,0:T(8,128)}, f32[64,128]{1,0:T(8,128)}, f32[32,128]{1,0:T(8,128)}) custom-call(f32[2,16,128]{2,1,0:T(8,128)} %get-tuple-element.16.beta_one, f32[2,16,128]{2,1,0:T(8,128)} %get-tuple-element.17.hat_one, f32[2,16,128]{2,1,0:T(8,128)} %get-tuple-element.19.beta_two, f32[2,16,128]{2,1,0:T(8,128)} %get-tuple-element.20.hat_two, ...), custom_call_target="tpu_custom_call" | custom-call | tf_op jit(solution)/shard_map/to_slots/pallas_call | solution.py:507
  111.0 0.0 copy-start
  111.0 1.4 %copy.24 = f32[2,4096]{1,0:T(2,128)} copy(f32[2,4096]{1,0:T(2,128)} %bitcast.38) | data formatting | bytes 65536
  112.4 0.0 copy-done
  112.4 0.0 copy-start.1
  112.4 0.6 copy.25
  113.0 0.1 copy-done.1
  113.1 0.6 copy.26
  (4 shorter events, 0.0 us)
Async XLA Ops:
  0.6 0.7 copy-start.5
  1.4 0.7 copy-start.4
  1.4 0.7 copy-start.3
  2.0 0.7 copy-start.2
  111.0 1.4 %copy-start = (f32[64,128]{1,0:T(8,128)S(1)}, f32[64,128]{1,0:T(8,128)}, u32[]{:S(2)}) copy-start(f32[64,128]{1,0:T(8,128)} %get-tuple-element.23) | copy-start | bytes 98308
  112.4 0.7 copy-start.1

commit v2 on v1

v2 whole, which is shorter than its diff:
```python
import functools
import math

import jax
import jax.numpy as jnp
from jax import lax
from jax.experimental import pallas as pl
from jax.experimental.pallas import tpu as pltpu
from jax.sharding import PartitionSpec as P

TX = 4
LANES = 128
PER = 16
NPIECE = 13
CHUNK = 64
NREGION = 8
NTILE = 32
F32 = jnp.float32
BF16 = jnp.bfloat16


def split3(x):
    hi = x.astype(BF16).astype(F32)
    rest = x - hi
    mid = rest.astype(BF16).astype(F32)
    low = (rest - mid).astype(BF16).astype(F32)
    return hi, mid, low


def wide_split(x):
    hi, mid, low = split3(x)
    return jnp.concatenate([hi.astype(BF16), mid.astype(BF16), low.astype(BF16)], axis=1)


def join3(x):
    return x[:, :LANES] + x[:, LANES : 2 * LANES] + x[:, 2 * LANES :]


def remote(src, dst, send, recv, region, tile):
    return pltpu.make_async_remote_copy(
        src_ref=src,
        dst_ref=dst,
        send_sem=send,
        recv_sem=recv,
        device_id=(region, tile),
        device_id_type=pl.DeviceIdType.MESH,
    )


def signal(sem, region, tile):
    pl.semaphore_signal(sem, inc=1, device_id=(region, tile), device_id_type=pl.DeviceIdType.MESH)


def each(low, high, step):
    def turn(index, carry):
        step(index)
        return carry

    lax.fori_loop(low, high, turn, 0)


def walk(tile):
    turned = (tile // 8) * 8 + 6 - lax.rem(tile, 8) + 2 * lax.rem(tile, 2)
    return jnp.where(lax.rem(tile // 8, 2) == 1, turned, tile)


def gather_kernel(
    offsets_in, design_in, target_in, prior_in, counts_in, width_in, reach_in, cells_in,
    data_out, width_out, list_out, cells_out, home_out,
    offs, design, target, prior, counts, widths, reach, cells, notes, rows_of,
    stage, rbuf, msg, recv, load, send1, recv1, send2, recv2,
):
    region = lax.axis_index("region")
    tile = lax.axis_index("tile")
    group = tile // 16
    piece = lax.rem(tile, 16)
    up = lax.rem(region + 1, NREGION)
    down = lax.rem(region + NREGION - 1, NREGION)

    barrier = pltpu.get_barrier_semaphore()
    each(1, NTILE, lambda o: signal(barrier, region, lax.rem(tile + o, NTILE)))
    each(0, 16, lambda i: signal(barrier, up, group * 16 + i))
    each(0, 16, lambda i: signal(barrier, down, group * 16 + i))

    loads = [
        pltpu.make_async_copy(source, place, load.at[k])
        for k, (source, place) in enumerate(
            (
                (counts_in, counts), (width_in, widths), (reach_in, reach), (cells_in, cells),
                (offsets_in, offs), (design_in, design), (target_in, target), (prior_in, prior),
            )
        )
    ]
    for copy in loads:
        copy.start()
    notes[...] = jnp.zeros((32, LANES), F32)
    stage[12] = jnp.zeros((24, LANES), F32)
    rows_of[...] = jnp.zeros((48, LANES), F32)
    for copy in loads[:4]:
        copy.wait()
    notes[0:1, 0:PER] = counts[...].astype(F32)
    notes[1:3, 0:PER] = widths[...].astype(F32)
    for e in range(9):
        for w in range(2):
            at = 3 + 9 * w + e
            notes[at : at + 1, 0:PER] = reach[e, w : w + 1, :].astype(F32)
    turned = jnp.transpose(notes[...])[0:PER]
    stage[12, 0:PER, 0:32] = turned
    cell = cells[...]
    order = (lax.bitwise_and(cell, 127) * TX + lax.shift_right_logical(cell, 7)).astype(F32)
    for k in range(8):
        notes[24:25, PER * k : PER * k + PER] = order
    row_lane = lax.broadcasted_iota(jnp.int32, (8, LANES), 1)
    cell_row = jnp.where(
        lax.shift_right_logical(row_lane, 4) == lax.rem(tile, 8),
        jnp.broadcast_to(notes[24:25, :], (8, LANES)), 0.0,
    )
    for p in range(NPIECE):
        stage[p, PER : PER + 8, :] = cell_row
    for copy in loads[4:]:
        copy.wait()
    lane = lax.broadcasted_iota(jnp.int32, (PER, LANES), 1)
    count = turned[:, 0:1]
    for t in range(PER):
        for h in range(2):
            span = slice(LANES * (2 * t + h), LANES * (2 * t + h + 1))
            for f in range(2):
                stage[2 * f + h, t : t + 1, :] = offs[f : f + 1, span]
                stage[4 + 4 * f + h, t : t + 1, :] = design[f : f + 1, span]
    for h in range(2):
        present = ((lane + LANES * h).astype(F32) < count).astype(F32)
        cov_one = stage[4 + h, 0:PER, :] * present
        cov_two = stage[8 + h, 0:PER, :]
        seen = target[pl.ds(h, PER, stride=2), :]
        before = prior[pl.ds(h, PER, stride=2), :]
        stage[4 + h, 0:PER, :] = cov_one
        stage[6 + h, 0:PER, :] = seen - cov_two * before
        cov_two = cov_two * present
        stage[8 + h, 0:PER, :] = cov_two
        stage[10 + h, 0:PER, :] = seen
        home_out[h] = cov_one
        home_out[2 + h] = cov_two
        home_out[4 + h] = seen * present

    pl.semaphore_wait(barrier, NTILE - 1 + 32)

    def to_middle(o):
        other = lax.rem(tile + o, NTILE)
        held = jnp.minimum(lax.rem(other, 16), NPIECE - 1)
        return remote(
            stage.at[held, pl.ds(0, PER + 1)], rbuf.at[tile, pl.ds(0, PER + 1)],
            send1.at[o], recv1.at[tile], region, other,
        )

    each(1, NTILE, lambda o: to_middle(o).start())
    rbuf[tile] = stage[jnp.minimum(piece, NPIECE - 1)]

    def from_source(o):
        other = lax.rem(tile + o, NTILE)
        return remote(
            stage.at[0, pl.ds(0, PER + 1)], rbuf.at[other, pl.ds(0, PER + 1)],
            send1.at[o], recv1.at[other], region, other,
        )

    each(1, NTILE, lambda o: from_source(o).wait_recv())

    cell_rows = [
        jnp.sum(rbuf[8 * b : 8 * b + 8, PER, :], axis=0, keepdims=True) for b in range(4)
    ]
    for b in range(4):
        cells_out[b : b + 1, :] = cell_rows[b]
    cells_out[4:8, :] = jnp.zeros((4, LANES), F32)

    @pl.when(piece < NPIECE)
    def _():
        spread = wide_split(rbuf[:, 0:PER, :].reshape(NTILE * PER, LANES))
        number = lax.broadcasted_iota(jnp.int32, (640, LANES), 0)
        owner = lax.shift_right_logical(number * 205, 13)
        q = number - owner * 40
        turned_owner = 14 - lax.bitwise_and(owner, 7) + 2 * lax.bitwise_and(owner, 1)
        first = (group * 16 + jnp.where(owner < 8, owner, turned_owner)) * 16
        side = jnp.where(q < 32, q - 24, q - 32)
        base = jnp.where(q < 24, q - 4, (side - 1) * 4 + jnp.where(q < 32, 3, 0))
        open_up = jnp.where(region < NREGION - 1, 1, 0)
        open_down = jnp.where(region > 0, 1, 0)
        beside = jnp.where(side < 6, jnp.where(q < 32, open_up, open_down), 0)
        allowed = jnp.where(q < 24, 1, beside)
        cell = first + base
        wanted = jnp.where(allowed > 0, cell, -1).astype(F32)
        hot = jnp.concatenate(
            [jnp.where(wanted == cell_rows[b], 1.0, 0.0).astype(BF16) for b in range(4)], axis=1
        )
        moved = join3(jnp.dot(hot, spread, preferred_element_type=F32))
        msg[...] = moved.reshape(16, 40, LANES)

    def own_copy(o):
        i = lax.rem(piece + o, 16)
        return remote(
            msg.at[i, pl.ds(0, 24)], recv.at[piece, pl.ds(0, 24)],
            send2.at[0, o], recv2.at[0, piece], region, group * 16 + i,
        )

    def up_copy(i):
        return remote(
            msg.at[i, pl.ds(24, 8)], recv.at[piece, pl.ds(24, 8)],
            send2.at[1, i], recv2.at[1, piece], up, group * 16 + i,
        )

    def down_copy(i):
        return remote(
            msg.at[i, pl.ds(32, 8)], recv.at[piece, pl.ds(32, 8)],
            send2.at[2, i], recv2.at[2, piece], down, group * 16 + i,
        )

    @pl.when(piece < NPIECE)
    def _():
        each(1, 16, lambda o: own_copy(o).start())
        each(0, 16, lambda i: up_copy(i).start())
        each(0, 16, lambda i: down_copy(i).start())
        recv[piece, 0:24, :] = msg[piece, 0:24, :]

    def wait_own(p):
        @pl.when(p != piece)
        def _():
            remote(
                msg.at[0, pl.ds(0, 24)], recv.at[p, pl.ds(0, 24)],
                send2.at[0, 0], recv2.at[0, p], region, group * 16 + p,
            ).wait_recv()

    def wait_sides(p):
        remote(
            msg.at[0, pl.ds(24, 8)], recv.at[p, pl.ds(24, 8)],
            send2.at[1, 0], recv2.at[1, p], down, group * 16 + p,
        ).wait_recv()
        remote(
            msg.at[0, pl.ds(32, 8)], recv.at[p, pl.ds(32, 8)],
            send2.at[2, 0], recv2.at[2, p], up, group * 16 + p,
        ).wait_recv()

    each(0, NPIECE, wait_own)
    each(0, NPIECE, wait_sides)
    for p in range(12):
        data_out[p] = recv[p]
    width_out[...] = recv[12, 4:20, :]
    for r in range(6):
        rows_of[8 * r : 8 * r + 1, :] = recv[12, 24 + r : 25 + r, :]
        rows_of[8 * r + 1 : 8 * r + 5, :] = recv[12, 4 * r : 4 * r + 4, :]
        rows_of[8 * r + 5 : 8 * r + 6, :] = recv[12, 32 + r : 33 + r, :]

    def spread_lane(r, at):
        return jnp.broadcast_to(rows_of[8 * r : 8 * r + 8, at : at + 1], (8, LANES))

    lanes = lax.broadcasted_iota(jnp.int32, (8, LANES), 1)
    lanes_f = lanes.astype(F32)
    over = lax.broadcasted_iota(jnp.int32, (8, LANES), 0)
    filled = [spread_lane(r, 0) for r in range(6)]
    near = [
        [filled[r] if a == 1 else pltpu.roll(filled[r], (1 - a) % 8, 0) for a in range(3)]
        for r in range(6)
    ]
    for w in range(2):
        for r in range(1, 5):
            many = jnp.zeros((8, LANES), F32)
            todo = jnp.zeros((8, LANES), F32)
            for e in range(9):
                beside, beyond = e // 3, r + e % 3 - 1
                there = near[beyond][beside]
                keep = None if e == 4 else spread_lane(r, 3 + 9 * w + e)
                c = over + (beside - 1)
                t = jnp.where(c == 0, 24 + beyond, jnp.where(c == 5, 32 + beyond, beyond * 4 + c - 1))
                at = (8 * t).astype(F32)
                for h in range(2):
                    flag = jnp.where(there > LANES * h, 1.0 if keep is None else keep, 0.0)
                    todo = todo + jnp.where(many == lanes_f, flag * (at + 320.0 * h), 0.0)
                    many = many + flag
            chunks = lax.shift_right_logical(filled[r].astype(jnp.int32) + CHUNK - 1, CHUNK.bit_length() - 1)
            value = jnp.where(lanes == 24, many, todo).astype(jnp.int32)
            value = jnp.where(lanes == 25, chunks, value)
            value = jnp.where(lanes == 26, filled[r].astype(jnp.int32), value)
            list_out[w, 8 * r - 8 : 8 * r, :] = value

    each(1, NTILE, lambda o: to_middle(o).wait_send())

    @pl.when(piece < NPIECE)
    def _():
        each(1, 16, lambda o: own_copy(o).wait_send())
        each(0, 16, lambda i: up_copy(i).wait_send())
        each(0, 16, lambda i: down_copy(i).wait_send())


def smooth_kernel(which, data, widths, lists, *refs):
    if which == 0:
        beta_out, hat_out, pull_out, *scratch = refs
    else:
        grid, beta_out, hat_out, *scratch = refs
    cand, square, fade, rates, fan, weight_sums, pull_sums, tall_of = scratch
    base = 32.0 * math.log2(math.e)
    width = widths[:, 1 + which : 2 + which]
    rate = jnp.broadcast_to(base / (width * width), (PER, LANES))
    rates[...] = -rate
    slot = lax.broadcasted_iota(jnp.int32, (40, LANES), 0)
    col = jnp.where(slot < 24, lax.rem(slot, 4) + 1, jnp.where(slot < 32, 0, 5)).astype(F32)
    row = jnp.where(
        slot < 24, slot // 4, jnp.where(slot < 32, slot - 24, slot - 32)
    ).astype(F32)

    def line(i):
        return lax.shift_right_logical(i, 2) * 8 + lax.bitwise_and(i, 3) + 1

    total = jnp.int32(0)
    for i in range(PER):
        at = 8 * (i // 4) + i % 4 + 1
        total = total + lists[which, at, 24] * lists[which, at, 25]

    columns = []
    for h in range(2):
        x = data[h] - 0.5
        y = data[2 + h] - 0.5
        cov = data[4 + 4 * which + h]
        squared = cov * cov
        square[h] = squared[4:20]
        pull = cov * data[6 + h] if which == 0 else grid[h]
        for k, field in enumerate((x + col, y + row, squared, pull)):
            cand[pl.ds(320 * h + k, 40, stride=8), :] = field
        own_x, own_y = x[4:20], y[4:20]
        fade[h] = jnp.exp2(-rate * (own_x * own_x + own_y * own_y))
        for source in (2.0 * rate * own_x, 2.0 * rate * own_y):
            columns.append(jnp.transpose(jnp.concatenate(split3(source), axis=0)).astype(BF16))
    columns = jnp.concatenate(columns, axis=0)
    which_row = lax.bitwise_and(lax.broadcasted_iota(jnp.int32, (3 * PER, LANES), 0), PER - 1)
    for i in range(PER):
        pick = jnp.where(which_row == i, 1.0, 0.0).astype(BF16)
        fan[i] = jnp.dot(columns, pick, preferred_element_type=F32)

    def item(n, carry):
        i, k, j, old_i, old_k, old_at, keep, power, weight_sum, pull_sum = carry
        weight = jnp.exp2(power)
        heavy = cand[pl.ds(old_at + 2, 1), :]
        drawn = cand[pl.ds(old_at + 3, 1), :]
        weight_sum = weight_sum * keep + weight * heavy
        pull_sum = pull_sum * keep + weight * drawn
        old = pl.ds(pl.multiple_of(old_k * CHUNK, CHUNK), CHUNK)
        weight_sums[old_i, old, :] = weight_sum
        pull_sums[old_i, old, :] = pull_sum

        here = line(i)
        at = lists[which, here, j]
        x = cand[pl.ds(at, 1), :] - (lax.bitwise_and(i, 3) + 1).astype(F32)
        y = cand[pl.ds(at + 1, 1), :] - (lax.shift_right_logical(i, 2) + 1).astype(F32)
        far = (x * x + y * y) * rates[pl.ds(i, 1), :]
        first = lax.shift_right_logical(k, 1) * 256 + lax.bitwise_and(k, 1) * CHUNK
        u = fan[i, pl.ds(pl.multiple_of(first, CHUNK), CHUNK), :]
        v = fan[i, pl.ds(pl.multiple_of(first + LANES, CHUNK), CHUNK), :]
        power = u * x + (v * y + far)
        keep = jnp.where(j == 0, 0.0, 1.0)
        last = j + 1 == lists[which, here, 24]
        end = last & (k + 1 == lists[which, here, 25])
        next_j = jnp.where(last, 0, j + 1)
        next_k = jnp.where(end, 0, jnp.where(last, k + 1, k))
        next_i = jnp.minimum(jnp.where(end, i + 1, i), PER - 1)
        return next_i, next_k, next_j, i, k, at, keep, power, weight_sum, pull_sum

    zero = fan[0, 0:CHUNK, :] * 0.0
    start = jnp.int32(0)
    lax.fori_loop(
        0, total + 1, item,
        (start, start, start, start, start, start, jnp.float32(0), zero, zero, zero),
    )

    ones = jnp.ones((8, LANES), BF16)
    lane = lax.broadcasted_iota(jnp.int32, (1, LANES), 1)

    def row_sum(values):
        high = values.astype(BF16)
        low = (values - high.astype(F32)).astype(BF16)
        both = jnp.concatenate([high, low], axis=0)
        sums = lax.dot_general(ones, both, (((1,), (1,)), ((), ())), preferred_element_type=F32)
        return sums[0:1, :LANES] + sums[0:1, LANES:]

    def finish(i, h):
        half = pl.ds(LANES * h, LANES)
        factor = fade[h, pl.ds(i, 1), :]
        total = 1.0 + factor * row_sum(weight_sums[i, half, :])
        drawn = factor * row_sum(pull_sums[i, half, :])
        live = lane + LANES * h < lists[which, line(i) if h else 8 * (i // 4) + i % 4 + 1, 26]
        beta = jnp.where(live, drawn / total, 0.0)
        beta_out[h, pl.ds(i, 1), :] = beta
        hat_out[h, pl.ds(i, 1), :] = jnp.where(live, square[h, pl.ds(i, 1), :] / total, 0.0)
        if which == 0:
            seen = data[10 + h, pl.ds(4 + i, 1), :]
            cov_one = data[4 + h, pl.ds(4 + i, 1), :]
            cov_two = data[8 + h, pl.ds(4 + i, 1), :]
            pull_out[h, pl.ds(i, 1), :] = cov_two * (seen - cov_one * beta)

    beta_out[1] = jnp.zeros((PER, LANES), F32)
    hat_out[1] = jnp.zeros((PER, LANES), F32)
    if which == 0:
        pull_out[1] = jnp.zeros((PER, LANES), F32)
    tall = jnp.int32(0)
    for i in range(PER):
        finish(i, 0)
        tall_of[tall] = i
        tall = tall + jnp.where(lists[which, 8 * (i // 4) + i % 4 + 1, 26] > LANES, 1, 0)

    def finish_some(g):
        for k in range(4):
            finish(tall_of[jnp.minimum(g * 4 + k, tall - 1)], 1)

    each(0, lax.shift_right_logical(tall + 3, 2), finish_some)


def halo_kernel(own, grid_out, recv, send, land):
    region = lax.axis_index("region")
    tile = lax.axis_index("tile")
    steps = [(a, b) for a in (-1, 0, 1) for b in (-1, 0, 1) if (a, b) != (0, 0)]

    owner = walk(tile)

    def place(a, b):
        return lax.rem(region + a + NREGION, NREGION), walk(lax.rem(owner + b + NTILE, NTILE))

    barrier = pltpu.get_barrier_semaphore()
    for a, b in steps:
        signal(barrier, *place(a, b))
    pl.semaphore_wait(barrier, 8)
    copies = []
    for k, (a, b) in enumerate(steps):
        copies.append(remote(own, recv.at[7 - k], send.at[k], land.at[7 - k], *place(a, b)))
    for copy in copies:
        copy.start()
    for copy in copies:
        copy.wait_recv()
    fits = {-1: region > 0, 0: None, 1: region < NREGION - 1}
    fits_row = {-1: owner > 0, 0: None, 1: owner < NTILE - 1}
    at = {step: k for k, step in enumerate(steps)}

    def take(h, a, b, low, high):
        rows = recv[at[(a, b)], h, low:high, :]
        for fit in (fits[a], fits_row[b]):
            if fit is not None:
                rows = jnp.where(fit, rows, 0.0)
        return rows

    for h in range(2):
        grid_out[h, 4:20, :] = own[h]
        grid_out[h, 0:4, :] = take(h, 0, -1, 12, 16)
        grid_out[h, 20:24, :] = take(h, 0, 1, 0, 4)
        for a, edge, first in ((-1, 3, 24), (1, 0, 32)):
            grid_out[h, first : first + 1, :] = take(h, a, -1, 12 + edge, 13 + edge)
            for r in range(4):
                grid_out[h, first + 1 + r : first + 2 + r, :] = take(h, a, 0, 4 * r + edge, 4 * r + edge + 1)
            grid_out[h, first + 5 : first + 6, :] = take(h, a, 1, edge, edge + 1)
            grid_out[h, first + 6 : first + 8, :] = jnp.zeros((2, LANES), F32)
    for copy in copies:
        copy.wait_send()


def return_kernel(
    beta_one, hat_one, beta_two, hat_two, cells, home, betas, hats, residual,
    stage, rbuf, msg, recv, send1, recv1, send2, recv2,
):
    region = lax.axis_index("region")
    tile = lax.axis_index("tile")
    group = tile // 8
    piece = lax.rem(tile, 8)
    barrier = pltpu.get_barrier_semaphore()
    each(1, NTILE, lambda o: signal(barrier, region, lax.rem(tile + o, NTILE)))
    for f, ref in enumerate((beta_one, hat_one, beta_two, hat_two)):
        for h in range(2):
            stage[2 * f + h] = ref[h]
    pl.semaphore_wait(barrier, NTILE - 1)

    def to_middle(o):
        other = lax.rem(tile + o, NTILE)
        return remote(
            stage.at[lax.rem(other, 8)], rbuf.at[tile], send1.at[o], recv1.at[tile], region, other
        )

    each(1, NTILE, lambda o: to_middle(o).start())
    rbuf[tile] = stage[piece]

    row = cells[pl.ds(group, 1), :]
    column = jnp.transpose(jnp.broadcast_to(row, (LANES, LANES)))
    lane = lax.broadcasted_iota(jnp.int32, (LANES, LANES), 1)
    hots = []
    for b in range(4):
        of = lax.shift_right_logical(lane, 4)
        if b % 2 == 1:
            of = 6 - of + 2 * lax.bitwise_and(of, 1)
        here = LANES * b + of * PER + lax.bitwise_and(lane, PER - 1)
        hots.append(jnp.where(here.astype(F32) == column, 1.0, 0.0).astype(BF16))
    hot = jnp.concatenate(hots, axis=1)

    def from_source(o):
        other = lax.rem(tile + o, NTILE)
        return remote(stage.at[0], rbuf.at[other], send1.at[o], recv1.at[other], region, other)

    each(1, NTILE, lambda o: from_source(o).wait_recv())
    spread = wide_split(rbuf[...].reshape(NTILE * PER, LANES))
    msg[...] = join3(jnp.dot(hot, spread, preferred_element_type=F32)).reshape(8, PER, LANES)

    def home_copy(o):
        i = lax.rem(piece + o, 8)
        return remote(
            msg.at[i], recv.at[piece], send2.at[o], recv2.at[piece], region, group * 8 + i
        )

    each(1, 8, lambda o: home_copy(o).start())
    recv[piece] = msg[piece]

    def from_middle(o):
        p = lax.rem(piece + o, 8)
        return remote(msg.at[0], recv.at[p], send2.at[o], recv2.at[p], region, group * 8 + p)

    each(1, 8, lambda o: from_middle(o).wait_recv())
    for h in range(2):
        left = home[4 + h] - home[h] * recv[h] - home[2 + h] * recv[4 + h]
        residual[pl.ds(h, PER, stride=2), :] = left
        for t in range(PER):
            span = slice(LANES * (2 * t + h), LANES * (2 * t + h + 1))
            for f in range(2):
                betas[f : f + 1, span] = recv[4 * f + h, t : t + 1, :]
                hats[f : f + 1, span] = recv[2 + 4 * f + h, t : t + 1, :]
    each(1, NTILE, lambda o: to_middle(o).wait_send())
    each(1, 8, lambda o: home_copy(o).wait_send())


def store_kernel(betas, hats, residual, betas_out, hats_out, residual_out, done):
    pairs = ((betas, betas_out), (hats, hats_out), (residual, residual_out))
    copies = [pltpu.make_async_copy(a, b, done.at[k]) for k, (a, b) in enumerate(pairs)]
    for copy in copies:
        copy.start()
    for copy in copies:
        copy.wait()


VM = pl.BlockSpec(memory_space=pltpu.VMEM)
SM = pl.BlockSpec(memory_space=pltpu.SMEM)
HB = pl.BlockSpec(memory_space=pltpu.HBM)
DMA = pltpu.SemaphoreType.DMA


def shape(*dims, dtype=F32):
    return jax.ShapeDtypeStruct(dims, dtype)


def smooth(which, data, widths, lists, *extra):
    outs = [shape(2, PER, LANES)] * (3 if which == 0 else 2)
    return pl.pallas_call(
        functools.partial(smooth_kernel, which),
        out_shape=outs,
        in_specs=[VM, VM, SM] + [VM] * len(extra),
        out_specs=[VM] * len(outs),
        scratch_shapes=[
            pltpu.VMEM((640, LANES), F32),
            pltpu.VMEM((2, PER, LANES), F32),
            pltpu.VMEM((2, PER, LANES), F32),
            pltpu.VMEM((PER, LANES), F32),
            pltpu.VMEM((PER, 4 * LANES, LANES), F32),
            pltpu.VMEM((PER, 2 * LANES, LANES), F32),
            pltpu.VMEM((PER, 2 * LANES, LANES), F32),
            pltpu.SMEM((32,), jnp.int32),
        ],
        compiler_params=pltpu.CompilerParams(vmem_limit_bytes=16 << 20),
        name="smooth_one" if which == 0 else "smooth_two",
    )(data, widths, lists, *extra)


def body(offsets, design, target, beta_second, counts, kernel_width, reach, assignment):
    data, widths, lists, cells, home = pl.pallas_call(
        gather_kernel,
        out_shape=[
            shape(12, 40, LANES), shape(PER, LANES), shape(2, 32, LANES, dtype=jnp.int32),
            shape(8, LANES), shape(6, PER, LANES),
        ],
        in_specs=[HB] * 8,
        out_specs=[VM] * 5,
        scratch_shapes=[
            pltpu.VMEM((2, NTILE * LANES), F32),
            pltpu.VMEM((2, NTILE * LANES), F32),
            pltpu.VMEM((NTILE, LANES), F32),
            pltpu.VMEM((NTILE, LANES), F32),
            pltpu.VMEM((1, PER), jnp.int32),
            pltpu.VMEM((2, PER), jnp.int32),
            pltpu.VMEM((9, 2, PER), jnp.int32),
            pltpu.VMEM((1, PER), jnp.int32),
            pltpu.VMEM((32, LANES), F32),
            pltpu.VMEM((48, LANES), F32),
            pltpu.VMEM((NPIECE, 24, LANES), F32),
            pltpu.VMEM((NTILE, 24, LANES), F32),
            pltpu.VMEM((16, 40, LANES), F32),
            pltpu.VMEM((NPIECE, 40, LANES), F32),
            DMA((8,)),
            DMA((NTILE,)),
            DMA((NTILE,)),
            DMA((3, 16)),
            DMA((3, 16)),
        ],
        compiler_params=pltpu.CompilerParams(collective_id=0, has_side_effects=True, vmem_limit_bytes=8 << 20),
        name="to_owners",
    )(
        *(
            pltpu.with_memory_space_constraint(value, pltpu.HBM)
            for value in (
                offsets, design, target.reshape(NTILE, LANES), beta_second.reshape(NTILE, LANES),
                counts.reshape(1, PER), kernel_width, reach.transpose(2, 0, 1), assignment,
            )
        )
    )
    beta_one, hat_one, pull = smooth(0, data, widths, lists)
    grid = pl.pallas_call(
        halo_kernel,
        out_shape=shape(2, 40, LANES),
        in_specs=[VM],
        out_specs=VM,
        scratch_shapes=[pltpu.VMEM((8, 2, PER, LANES), F32), DMA((8,)), DMA((8,))],
        compiler_params=pltpu.CompilerParams(collective_id=1, has_side_effects=True, vmem_limit_bytes=8 << 20),
        name="edges",
    )(pull)
    beta_two, hat_two = smooth(1, data, widths, lists, grid)
    betas, hats, residual = pl.pallas_call(
        return_kernel,
        out_shape=[shape(2, NTILE * LANES), shape(2, NTILE * LANES), shape(NTILE, LANES)],
        in_specs=[VM] * 6,
        out_specs=[VM] * 3,
        scratch_shapes=[
            pltpu.VMEM((8, PER, LANES), F32),
            pltpu.VMEM((NTILE, PER, LANES), F32),
            pltpu.VMEM((8, PER, LANES), F32),
            pltpu.VMEM((8, PER, LANES), F32),
            DMA((NTILE,)),
            DMA((NTILE,)),
            DMA((8,)),
            DMA((8,)),
        ],
        compiler_params=pltpu.CompilerParams(collective_id=2, has_side_effects=True, vmem_limit_bytes=8 << 20),
        name="to_slots",
    )(beta_one, hat_one, beta_two, hat_two, cells, home)
    betas, hats, residual = pl.pallas_call(
        store_kernel,
        out_shape=[shape(2, NTILE * LANES), shape(2, NTILE * LANES), shape(NTILE, LANES)],
        in_specs=[VM] * 3,
        out_specs=[HB] * 3,
        scratch_shapes=[DMA((3,))],
        compiler_params=pltpu.CompilerParams(vmem_limit_bytes=8 << 20),
        name="store",
    )(betas, hats, residual)
    return betas, hats, residual.reshape(-1)


def solution(mesh):
    split = ("region", "tile")
    in_specs = (
        P(None, split), P(None, split), P(split), P(split), P(split), P(None, split),
        P(None, split, None), P("region", "tile"),
    )
    out_specs = (P(None, split), P(None, split), P(split))
    return jax.shard_map(body, mesh=mesh, in_specs=in_specs, out_specs=out_specs, check_vma=False)
```

time: 114 us -> 66.1 us (0.58)
  Pallas kernels: 107 us -> 64.5 us
  local copies, waits for them, and re-layouts: 4.97 us -> 0 us
    pallas_call x2, Pallas kernels: 54.1 us -> 14.7 us  [smooth(): pl.pallas_call(functools.partial(smooth_kernel, which), out_shape=outs, i...]
    unnamed x18 -> x0, local copies, waits for them, and re-layouts: 4.79 us -> none
    pallas_call x2 -> x3, Pallas kernels: 46.3 us -> 43.9 us  [the longest x1 27 us: body(): pl.pallas_call(gather_kernel, out_shape=[shape(12, 40, LANES), shape(PER,...]
where the time goes in v2:
time: 66.1 us; the launch traced here: 65.1 us
  Pallas kernels  64.5 us (98%)
  between operations  0.67 us (1%)
    pallas_call x1, Pallas kernels, body(): pl.pallas_call(gather_kernel, out_shape=[shape(12, 40, LANES), shape(PER,...  27 us
    pallas_call x1, Pallas kernels, body(): pl.pallas_call(return_kernel, out_shape=[shape(2, NTILE * LANES), shape(2...  16.2 us
    pallas_call x2, Pallas kernels, smooth(): pl.pallas_call(functools.partial(smooth_kernel, which), out_shape=outs, i...  14.7 us
    pallas_call x1, Pallas kernels, body(): pl.pallas_call(halo_kernel, out_shape=shape(2, 40, LANES), in_specs=[VM],...  5.82 us

profile of v2, /device:TPU:1, one launch (start us, length us, event | category | flops | bytes accessed | tf_op | source)
XLA Modules:
  0.0 65.1 jit_solution(5601906546161584434)
XLA Ops:
  0.6 27.0 %to_owners.1 = (f32[12,40,128]{2,1,0:T(8,128)S(1)}, f32[16,128]{1,0:T(8,128)S(1)}, s32[2,32,128]{2,1,0:T(8,128)S(1)}, f32[8,128]{1,0:T(8,128)S(1)}, f32[6,16,128]{2,1,0:T(8,128)S(1)}) custom-call(f32[2,4096]{1,0:T(2,128)} %offsets_in.1, f32[2,4096]{1,0:T(2,128)} %design_in.1, f32[32,128]{1,0:T(8,128)} %bitcast.5, f32[32,128]{1,0:T(8,128)} %bitcast.6, ...), custom_call_target="tpu_custom_call" | custom-call | tf_op jit(solution)/shard_map/to_owners/pallas_call | solution.py:570
  27.7 7.7 %smooth_one.1 = (f32[2,16,128]{2,1,0:T(8,128)S(1)}, f32[2,16,128]{2,1,0:T(8,128)S(1)}, f32[2,16,128]{2,1,0:T(8,128)S(1)}) custom-call(f32[12,40,128]{2,1,0:T(8,128)S(1)} %get-tuple-element.19.data, f32[16,128]{1,0:T(8,128)S(1)} %get-tuple-element.20.widths, s32[2,32,128]{2,1,0:T(8,128)S(1)} %get-tuple-element.21.lists), custom_call_target="tpu_custom_call" | custom-call | tf_op jit(solution)/shard_map/smooth_one/pallas_call | solution.py:549
  35.4 5.8 %edges.1.refs_0_ = f32[2,40,128]{2,1,0:T(8,128)S(1)} custom-call(f32[2,16,128]{2,1,0:T(8,128)S(1)} %get-tuple-element.24.own), custom_call_target="tpu_custom_call" | custom-call | tf_op jit(solution)/shard_map/edges/pallas_call | solution.py:611
  41.2 7.0 %smooth_two.1 = (f32[2,16,128]{2,1,0:T(8,128)S(1)}, f32[2,16,128]{2,1,0:T(8,128)S(1)}) custom-call(f32[12,40,128]{2,1,0:T(8,128)S(1)} %get-tuple-element.19.data, f32[16,128]{1,0:T(8,128)S(1)} %get-tuple-element.20.widths, s32[2,32,128]{2,1,0:T(8,128)S(1)} %get-tuple-element.21.lists, f32[2,40,128]{2,1,0:T(8,128)S(1)} %edges.1.refs_0_), custom_call_target="tpu_custom_call" | custom-call | tf_op jit(solution)/shard_map/smooth_two/pallas_call | solution.py:549
  48.3 16.2 %to_slots.1 = (f32[2,4096]{1,0:T(2,128)S(1)}, f32[2,4096]{1,0:T(2,128)S(1)}, f32[32,128]{1,0:T(8,128)S(1)}) custom-call(f32[2,16,128]{2,1,0:T(8,128)S(1)} %get-tuple-element.22.beta_one, f32[2,16,128]{2,1,0:T(8,128)S(1)} %get-tuple-element.23.hat_one, f32[2,16,128]{2,1,0:T(8,128)S(1)} %get-tuple-element.25.beta_two, ...), custom_call_target="tpu_custom_call" | custom-call | tf_op jit(solution)/shard_map/to_slots/pallas_call | solution.py:621
  64.5 0.7 %store.1 = (f32[2,4096]{1,0:T(2,128)}, f32[2,4096]{1,0:T(2,128)}, f32[32,128]{1,0:T(8,128)}) custom-call(f32[2,4096]{1,0:T(2,128)S(1)} %get-tuple-element.29.betas, f32[2,4096]{1,0:T(2,128)S(1)} %get-tuple-element.30.hats, f32[32,128]{1,0:T(8,128)S(1)} %get-tuple-element.31.residual), custom_call_target="tpu_custom_call" | custom-call | tf_op jit(solution)/shard_map/store/pallas_call | solution.py:639

commit v3 on v2

--- a/solution.py
+++ b/solution.py
@@ -68,7 +68,7 @@
     offsets_in, design_in, target_in, prior_in, counts_in, width_in, reach_in, cells_in,
     data_out, width_out, list_out, cells_out, home_out,
     offs, design, target, prior, counts, widths, reach, cells, notes, rows_of,
-    stage, rbuf, msg, recv, load, send1, recv1, send2, recv2,
+    wanted, stage, rbuf, msg, recv, load, send1, recv1, send2, recv2,
 ):
     region = lax.axis_index("region")
     tile = lax.axis_index("tile")
@@ -155,6 +155,20 @@
     each(1, NTILE, lambda o: to_middle(o).start())
     rbuf[tile] = stage[jnp.minimum(piece, NPIECE - 1)]
 
+    number = lax.broadcasted_iota(jnp.int32, (640, LANES), 0)
+    owner = lax.shift_right_logical(number * 205, 13)
+    q = number - owner * 40
+    turned_owner = 14 - lax.bitwise_and(owner, 7) + 2 * lax.bitwise_and(owner, 1)
+    first = (group * 16 + jnp.where(owner < 8, owner, turned_owner)) * 16
+    side = jnp.where(q < 32, q - 24, q - 32)
+    base = jnp.where(q < 24, q - 4, (side - 1) * 4 + jnp.where(q < 32, 3, 0))
+    open_up = jnp.where(region < NREGION - 1, 1, 0)
+    open_down = jnp.where(region > 0, 1, 0)
+    beside = jnp.where(side < 6, jnp.where(q < 32, open_up, open_down), 0)
+    allowed = jnp.where(q < 24, 1, beside)
+    cell = first + base
+    wanted[...] = jnp.where(allowed > 0, cell, -1).astype(F32)
+
     def from_source(o):
         other = lax.rem(tile + o, NTILE)
         return remote(
@@ -174,21 +188,8 @@
     @pl.when(piece < NPIECE)
     def _():
         spread = wide_split(rbuf[:, 0:PER, :].reshape(NTILE * PER, LANES))
-        number = lax.broadcasted_iota(jnp.int32, (640, LANES), 0)
-        owner = lax.shift_right_logical(number * 205, 13)
-        q = number - owner * 40
-        turned_owner = 14 - lax.bitwise_and(owner, 7) + 2 * lax.bitwise_and(owner, 1)
-        first = (group * 16 + jnp.where(owner < 8, owner, turned_owner)) * 16
-        side = jnp.where(q < 32, q - 24, q - 32)
-        base = jnp.where(q < 24, q - 4, (side - 1) * 4 + jnp.where(q < 32, 3, 0))
-        open_up = jnp.where(region < NREGION - 1, 1, 0)
-        open_down = jnp.where(region > 0, 1, 0)
-        beside = jnp.where(side < 6, jnp.where(q < 32, open_up, open_down), 0)
-        allowed = jnp.where(q < 24, 1, beside)
-        cell = first + base
-        wanted = jnp.where(allowed > 0, cell, -1).astype(F32)
         hot = jnp.concatenate(
-            [jnp.where(wanted == cell_rows[b], 1.0, 0.0).astype(BF16) for b in range(4)], axis=1
+            [jnp.where(wanted[...] == cell_rows[b], 1.0, 0.0).astype(BF16) for b in range(4)], axis=1
         )
         moved = join3(jnp.dot(hot, spread, preferred_element_type=F32))
         msg[...] = moved.reshape(16, 40, LANES)
@@ -274,7 +275,9 @@
                     todo = todo + jnp.where(many == lanes_f, flag * (at + 320.0 * h), 0.0)
                     many = many + flag
             chunks = lax.shift_right_logical(filled[r].astype(jnp.int32) + CHUNK - 1, CHUNK.bit_length() - 1)
-            value = jnp.where(lanes == 24, many, todo).astype(jnp.int32)
+            value = jnp.where(lanes_f < many, todo, 240.0).astype(jnp.int32)
+            pairs = lax.shift_right_logical(many.astype(jnp.int32) + 1, 1)
+            value = jnp.where(lanes == 24, pairs, value)
             value = jnp.where(lanes == 25, chunks, value)
             value = jnp.where(lanes == 26, filled[r].astype(jnp.int32), value)
             list_out[w, 8 * r - 8 : 8 * r, :] = value
@@ -288,43 +291,27 @@
         each(0, 16, lambda i: down_copy(i).wait_send())
 
 
-def smooth_kernel(which, data, widths, lists, *refs):
-    if which == 0:
-        beta_out, hat_out, pull_out, *scratch = refs
-    else:
-        grid, beta_out, hat_out, *scratch = refs
-    cand, square, fade, rates, fan, weight_sums, pull_sums, tall_of = scratch
-    base = 32.0 * math.log2(math.e)
-    width = widths[:, 1 + which : 2 + which]
-    rate = jnp.broadcast_to(base / (width * width), (PER, LANES))
+def rate_of(which, notes):
+    width = notes[:, 1 + which : 2 + which]
+    return jnp.broadcast_to((32.0 * math.log2(math.e)) / (width * width), (PER, LANES))
+
+
+def prepare(which, data, notes, cand, fan, rates):
+    rate = rate_of(which, notes)
     rates[...] = -rate
     slot = lax.broadcasted_iota(jnp.int32, (40, LANES), 0)
     col = jnp.where(slot < 24, lax.rem(slot, 4) + 1, jnp.where(slot < 32, 0, 5)).astype(F32)
     row = jnp.where(
         slot < 24, slot // 4, jnp.where(slot < 32, slot - 24, slot - 32)
     ).astype(F32)
-
-    def line(i):
-        return lax.shift_right_logical(i, 2) * 8 + lax.bitwise_and(i, 3) + 1
-
-    total = jnp.int32(0)
-    for i in range(PER):
-        at = 8 * (i // 4) + i % 4 + 1
-        total = total + lists[which, at, 24] * lists[which, at, 25]
-
     columns = []
     for h in range(2):
         x = data[h] - 0.5
         y = data[2 + h] - 0.5
         cov = data[4 + 4 * which + h]
-        squared = cov * cov
-        square[h] = squared[4:20]
-        pull = cov * data[6 + h] if which == 0 else grid[h]
-        for k, field in enumerate((x + col, y + row, squared, pull)):
+        for k, field in enumerate((x + col, y + row, cov * cov)):
             cand[pl.ds(320 * h + k, 40, stride=8), :] = field
-        own_x, own_y = x[4:20], y[4:20]
-        fade[h] = jnp.exp2(-rate * (own_x * own_x + own_y * own_y))
-        for source in (2.0 * rate * own_x, 2.0 * rate * own_y):
+        for source in (2.0 * rate * x[4:20], 2.0 * rate * y[4:20]):
             columns.append(jnp.transpose(jnp.concatenate(split3(source), axis=0)).astype(BF16))
     columns = jnp.concatenate(columns, axis=0)
     which_row = lax.bitwise_and(lax.broadcasted_iota(jnp.int32, (3 * PER, LANES), 0), PER - 1)
@@ -332,84 +319,106 @@
         pick = jnp.where(which_row == i, 1.0, 0.0).astype(BF16)
         fan[i] = jnp.dot(columns, pick, preferred_element_type=F32)
 
+
+def sums_of(which, cand, pull, fan, rates, lists, weight_sums, pull_sums):
+    def line(i):
+        return lax.shift_right_logical(i, 2) * 8 + lax.bitwise_and(i, 3) + 1
+
+    total = jnp.int32(0)
+    for i in range(PER):
+        at = 8 * (i // 4) + i % 4 + 1
+        total = total + lists[which, at, 24] * lists[which, at, 25]
+
+    shape3 = (CHUNK // 8, 8, LANES)
+
+    def row(ref, at):
+        return jnp.broadcast_to(ref[pl.ds(at, 1), :], (8, LANES))
+
     def item(n, carry):
-        i, k, j, old_i, old_k, old_at, keep, power, weight_sum, pull_sum = carry
-        weight = jnp.exp2(power)
-        heavy = cand[pl.ds(old_at + 2, 1), :]
-        drawn = cand[pl.ds(old_at + 3, 1), :]
-        weight_sum = weight_sum * keep + weight * heavy
-        pull_sum = pull_sum * keep + weight * drawn
+        i, k, j, at, pairs, chunks, old_i, old_k, old_at, keep, powers, sums = carry
+        sums = [value * keep for value in sums]
+        for power, base in zip(powers, old_at):
+            weight = jnp.exp2(power)
+            sums[0] = sums[0] + weight * row(cand, base + 2)
+            sums[1] = sums[1] + weight * row(pull, lax.shift_right_logical(base, 3))
         old = pl.ds(pl.multiple_of(old_k * CHUNK, CHUNK), CHUNK)
-        weight_sums[old_i, old, :] = weight_sum
-        pull_sums[old_i, old, :] = pull_sum
-
-        here = line(i)
-        at = lists[which, here, j]
-        x = cand[pl.ds(at, 1), :] - (lax.bitwise_and(i, 3) + 1).astype(F32)
-        y = cand[pl.ds(at + 1, 1), :] - (lax.shift_right_logical(i, 2) + 1).astype(F32)
-        far = (x * x + y * y) * rates[pl.ds(i, 1), :]
+        weight_sums[old_i, old, :] = sums[0].reshape(CHUNK, LANES)
+        pull_sums[old_i, old, :] = sums[1].reshape(CHUNK, LANES)
+
         first = lax.shift_right_logical(k, 1) * 256 + lax.bitwise_and(k, 1) * CHUNK
-        u = fan[i, pl.ds(pl.multiple_of(first, CHUNK), CHUNK), :]
-        v = fan[i, pl.ds(pl.multiple_of(first + LANES, CHUNK), CHUNK), :]
-        power = u * x + (v * y + far)
+        u = fan[i, pl.ds(pl.multiple_of(first, CHUNK), CHUNK), :].reshape(shape3)
+        v = fan[i, pl.ds(pl.multiple_of(first + LANES, CHUNK), CHUNK), :].reshape(shape3)
+        scale = row(rates, i)
+        shift_x = (lax.bitwise_and(i, 3) + 1).astype(F32)
+        shift_y = (lax.shift_right_logical(i, 2) + 1).astype(F32)
+        powers = []
+        for base in at:
+            x = row(cand, base) - shift_x
+            y = row(cand, base + 1) - shift_y
+            powers.append(u * x + (v * y + (x * x + y * y) * scale))
         keep = jnp.where(j == 0, 0.0, 1.0)
-        last = j + 1 == lists[which, here, 24]
-        end = last & (k + 1 == lists[which, here, 25])
+        last = j + 1 == pairs
+        end = last & (k + 1 == chunks)
         next_j = jnp.where(last, 0, j + 1)
         next_k = jnp.where(end, 0, jnp.where(last, k + 1, k))
         next_i = jnp.minimum(jnp.where(end, i + 1, i), PER - 1)
-        return next_i, next_k, next_j, i, k, at, keep, power, weight_sum, pull_sum
-
-    zero = fan[0, 0:CHUNK, :] * 0.0
+        here = line(next_i)
+        return (
+            next_i, next_k, next_j,
+            (lists[which, here, 2 * next_j], lists[which, here, 2 * next_j + 1]),
+            lists[which, here, 24], lists[which, here, 25], i, k, at, keep, tuple(powers), tuple(sums),
+        )
+
+    zero = (fan[0, 0:CHUNK, :] * 0.0).reshape(shape3)
     start = jnp.int32(0)
     lax.fori_loop(
         0, total + 1, item,
-        (start, start, start, start, start, start, jnp.float32(0), zero, zero, zero),
+        (
+            start, start, start, (lists[which, 1, 0], lists[which, 1, 1]),
+            lists[which, 1, 24], lists[which, 1, 25],
+            start, start, (start, start), jnp.float32(0), (zero, zero), (zero, zero),
+        ),
     )
 
+
+def first_kernel(data, notes, lists, weight_sums, pull_sums, cand, pull, fan, rates):
+    prepare(0, data, notes, cand, fan, rates)
+    for h in range(2):
+        pull[40 * h : 40 * h + 40, :] = data[4 + h] * data[6 + h]
+    sums_of(0, cand, pull, fan, rates, lists, weight_sums, pull_sums)
+
+
+def second_kernel(cand, pull, fan, rates, lists, weight_sums, pull_sums):
+    sums_of(1, cand, pull, fan, rates, lists, weight_sums, pull_sums)
+
+
+def finish(which, h, data, notes, weight_sums, pull_sums, totals):
     ones = jnp.ones((8, LANES), BF16)
-    lane = lax.broadcasted_iota(jnp.int32, (1, LANES), 1)
-
-    def row_sum(values):
-        high = values.astype(BF16)
-        low = (values - high.astype(F32)).astype(BF16)
-        both = jnp.concatenate([high, low], axis=0)
-        sums = lax.dot_general(ones, both, (((1,), (1,)), ((), ())), preferred_element_type=F32)
-        return sums[0:1, :LANES] + sums[0:1, LANES:]
-
-    def finish(i, h):
-        half = pl.ds(LANES * h, LANES)
-        factor = fade[h, pl.ds(i, 1), :]
-        total = 1.0 + factor * row_sum(weight_sums[i, half, :])
-        drawn = factor * row_sum(pull_sums[i, half, :])
-        live = lane + LANES * h < lists[which, line(i) if h else 8 * (i // 4) + i % 4 + 1, 26]
-        beta = jnp.where(live, drawn / total, 0.0)
-        beta_out[h, pl.ds(i, 1), :] = beta
-        hat_out[h, pl.ds(i, 1), :] = jnp.where(live, square[h, pl.ds(i, 1), :] / total, 0.0)
-        if which == 0:
-            seen = data[10 + h, pl.ds(4 + i, 1), :]
-            cov_one = data[4 + h, pl.ds(4 + i, 1), :]
-            cov_two = data[8 + h, pl.ds(4 + i, 1), :]
-            pull_out[h, pl.ds(i, 1), :] = cov_two * (seen - cov_one * beta)
-
-    beta_out[1] = jnp.zeros((PER, LANES), F32)
-    hat_out[1] = jnp.zeros((PER, LANES), F32)
-    if which == 0:
-        pull_out[1] = jnp.zeros((PER, LANES), F32)
-    tall = jnp.int32(0)
-    for i in range(PER):
-        finish(i, 0)
-        tall_of[tall] = i
-        tall = tall + jnp.where(lists[which, 8 * (i // 4) + i % 4 + 1, 26] > LANES, 1, 0)
-
-    def finish_some(g):
-        for k in range(4):
-            finish(tall_of[jnp.minimum(g * 4 + k, tall - 1)], 1)
-
-    each(0, lax.shift_right_logical(tall + 3, 2), finish_some)
-
-
-def halo_kernel(own, grid_out, recv, send, land):
+    for k, ref in enumerate((weight_sums, pull_sums)):
+        for i in range(PER):
+            values = ref[i, LANES * h : LANES * h + LANES, :]
+            high = values.astype(BF16)
+            low = (values - high.astype(F32)).astype(BF16)
+            both = jnp.concatenate([high, low], axis=0)
+            sums = lax.dot_general(
+                ones, both, (((1,), (1,)), ((), ())), preferred_element_type=F32
+            )
+            totals[k, i : i + 1, :] = sums[0:1, :LANES] + sums[0:1, LANES:]
+    x = data[h, 4:20, :] - 0.5
+    y = data[2 + h, 4:20, :] - 0.5
+    cov = data[4 + 4 * which + h, 4:20, :]
+    fade = jnp.exp2(-rate_of(which, notes) * (x * x + y * y))
+    lane = lax.broadcasted_iota(jnp.int32, (PER, LANES), 1)
+    live = (lane + LANES * h).astype(F32) < notes[:, 0:1]
+    total = 1.0 + fade * totals[0]
+    beta = jnp.where(live, fade * totals[1] / total, 0.0)
+    return beta, jnp.where(live, cov * cov / total, 0.0)
+
+
+def halo_kernel(
+    weight_sums, pull_sums, data, notes, grid_out, beta_out, hat_out, cand_out, fan_out, rates_out,
+    own, totals, recv, send, land,
+):
     region = lax.axis_index("region")
     tile = lax.axis_index("tile")
     steps = [(a, b) for a in (-1, 0, 1) for b in (-1, 0, 1) if (a, b) != (0, 0)]
@@ -422,12 +431,18 @@
     barrier = pltpu.get_barrier_semaphore()
     for a, b in steps:
         signal(barrier, *place(a, b))
+    for h in range(2):
+        beta, hat = finish(0, h, data, notes, weight_sums, pull_sums, totals)
+        beta_out[h] = beta
+        hat_out[h] = hat
+        own[h] = data[8 + h, 4:20, :] * (data[10 + h, 4:20, :] - data[4 + h, 4:20, :] * beta)
     pl.semaphore_wait(barrier, 8)
     copies = []
     for k, (a, b) in enumerate(steps):
         copies.append(remote(own, recv.at[7 - k], send.at[k], land.at[7 - k], *place(a, b)))
     for copy in copies:
         copy.start()
+    prepare(1, data, notes, cand_out, fan_out, rates_out)
     for copy in copies:
         copy.wait_recv()
     fits = {-1: region > 0, 0: None, 1: region < NREGION - 1}
@@ -442,22 +457,23 @@
         return rows
 
     for h in range(2):
-        grid_out[h, 4:20, :] = own[h]
-        grid_out[h, 0:4, :] = take(h, 0, -1, 12, 16)
-        grid_out[h, 20:24, :] = take(h, 0, 1, 0, 4)
-        for a, edge, first in ((-1, 3, 24), (1, 0, 32)):
-            grid_out[h, first : first + 1, :] = take(h, a, -1, 12 + edge, 13 + edge)
+        to = 40 * h
+        grid_out[to + 4 : to + 20, :] = own[h]
+        grid_out[to : to + 4, :] = take(h, 0, -1, 12, 16)
+        grid_out[to + 20 : to + 24, :] = take(h, 0, 1, 0, 4)
+        for a, edge, first in ((-1, 3, to + 24), (1, 0, to + 32)):
+            grid_out[first : first + 1, :] = take(h, a, -1, 12 + edge, 13 + edge)
             for r in range(4):
-                grid_out[h, first + 1 + r : first + 2 + r, :] = take(h, a, 0, 4 * r + edge, 4 * r + edge + 1)
-            grid_out[h, first + 5 : first + 6, :] = take(h, a, 1, edge, edge + 1)
-            grid_out[h, first + 6 : first + 8, :] = jnp.zeros((2, LANES), F32)
+                grid_out[first + 1 + r : first + 2 + r, :] = take(h, a, 0, 4 * r + edge, 4 * r + edge + 1)
+            grid_out[first + 5 : first + 6, :] = take(h, a, 1, edge, edge + 1)
+            grid_out[first + 6 : first + 8, :] = jnp.zeros((2, LANES), F32)
     for copy in copies:
         copy.wait_send()
 
 
 def return_kernel(
-    beta_one, hat_one, beta_two, hat_two, cells, home, betas, hats, residual,
-    stage, rbuf, msg, recv, send1, recv1, send2, recv2,
+    beta_one, hat_one, weight_sums, pull_sums, data, notes, cells, home, betas, hats, residual,
+    totals, stage, rbuf, msg, recv, send1, recv1, send2, recv2,
 ):
     region = lax.axis_index("region")
     tile = lax.axis_index("tile")
@@ -465,9 +481,10 @@
     piece = lax.rem(tile, 8)
     barrier = pltpu.get_barrier_semaphore()
     each(1, NTILE, lambda o: signal(barrier, region, lax.rem(tile + o, NTILE)))
-    for f, ref in enumerate((beta_one, hat_one, beta_two, hat_two)):
-        for h in range(2):
-            stage[2 * f + h] = ref[h]
+    for h in range(2):
+        stage[h] = beta_one[h]
+        stage[2 + h] = hat_one[h]
+        stage[4 + h], stage[6 + h] = finish(1, h, data, notes, weight_sums, pull_sums, totals)
     pl.semaphore_wait(barrier, NTILE - 1)
 
     def to_middle(o):
@@ -544,30 +561,8 @@
     return jax.ShapeDtypeStruct(dims, dtype)
 
 
-def smooth(which, data, widths, lists, *extra):
-    outs = [shape(2, PER, LANES)] * (3 if which == 0 else 2)
-    return pl.pallas_call(
-        functools.partial(smooth_kernel, which),
-        out_shape=outs,
-        in_specs=[VM, VM, SM] + [VM] * len(extra),
-        out_specs=[VM] * len(outs),
-        scratch_shapes=[
-            pltpu.VMEM((640, LANES), F32),
-            pltpu.VMEM((2, PER, LANES), F32),
-            pltpu.VMEM((2, PER, LANES), F32),
-            pltpu.VMEM((PER, LANES), F32),
-            pltpu.VMEM((PER, 4 * LANES, LANES), F32),
-            pltpu.VMEM((PER, 2 * LANES, LANES), F32),
-            pltpu.VMEM((PER, 2 * LANES, LANES), F32),
-            pltpu.SMEM((32,), jnp.int32),
-        ],
-        compiler_params=pltpu.CompilerParams(vmem_limit_bytes=16 << 20),
-        name="smooth_one" if which == 0 else "smooth_two",
-    )(data, widths, lists, *extra)
-
-
 def body(offsets, design, target, beta_second, counts, kernel_width, reach, assignment):
-    data, widths, lists, cells, home = pl.pallas_call(
+    data, notes, lists, cells, home = pl.pallas_call(
         gather_kernel,
         out_shape=[
             shape(12, 40, LANES), shape(PER, LANES), shape(2, 32, LANES, dtype=jnp.int32),
@@ -586,6 +581,7 @@
             pltpu.VMEM((1, PER), jnp.int32),
             pltpu.VMEM((32, LANES), F32),
             pltpu.VMEM((48, LANES), F32),
+            pltpu.VMEM((640, LANES), F32),
             pltpu.VMEM((NPIECE, 24, LANES), F32),
             pltpu.VMEM((NTILE, 24, LANES), F32),
             pltpu.VMEM((16, 40, LANES), F32),
@@ -607,23 +603,52 @@
             )
         )
     )
-    beta_one, hat_one, pull = smooth(0, data, widths, lists)
-    grid = pl.pallas_call(
+    sums = [shape(PER, 2 * LANES, LANES)] * 2
+    tables = [(640, LANES), (80, LANES), (PER, 4 * LANES, LANES), (PER, LANES)]
+    weight_sums, pull_sums = pl.pallas_call(
+        first_kernel,
+        out_shape=sums,
+        in_specs=[VM, VM, SM],
+        out_specs=[VM] * 2,
+        scratch_shapes=[pltpu.VMEM(dims, F32) for dims in tables],
+        compiler_params=pltpu.CompilerParams(vmem_limit_bytes=16 << 20),
+        name="smooth_one",
+    )(data, notes, lists)
+    grid, beta_one, hat_one, cand, fan, rates = pl.pallas_call(
         halo_kernel,
-        out_shape=shape(2, 40, LANES),
-        in_specs=[VM],
-        out_specs=VM,
-        scratch_shapes=[pltpu.VMEM((8, 2, PER, LANES), F32), DMA((8,)), DMA((8,))],
-        compiler_params=pltpu.CompilerParams(collective_id=1, has_side_effects=True, vmem_limit_bytes=8 << 20),
+        out_shape=[
+            shape(80, LANES), shape(2, PER, LANES), shape(2, PER, LANES), shape(640, LANES),
+            shape(PER, 4 * LANES, LANES), shape(PER, LANES),
+        ],
+        in_specs=[VM] * 4,
+        out_specs=[VM] * 6,
+        scratch_shapes=[
+            pltpu.VMEM((2, PER, LANES), F32),
+            pltpu.VMEM((2, PER, LANES), F32),
+            pltpu.VMEM((8, 2, PER, LANES), F32),
+            DMA((8,)),
+            DMA((8,)),
+        ],
+        compiler_params=pltpu.CompilerParams(
+            collective_id=1, has_side_effects=True, vmem_limit_bytes=16 << 20
+        ),
         name="edges",
-    )(pull)
-    beta_two, hat_two = smooth(1, data, widths, lists, grid)
+    )(weight_sums, pull_sums, data, notes)
+    weight_sums, pull_sums = pl.pallas_call(
+        second_kernel,
+        out_shape=sums,
+        in_specs=[VM] * 4 + [SM],
+        out_specs=[VM] * 2,
+        compiler_params=pltpu.CompilerParams(vmem_limit_bytes=16 << 20),
+        name="smooth_two",
+    )(cand, grid, fan, rates, lists)
     betas, hats, residual = pl.pallas_call(
         return_kernel,
         out_shape=[shape(2, NTILE * LANES), shape(2, NTILE * LANES), shape(NTILE, LANES)],
-        in_specs=[VM] * 6,
+        in_specs=[VM] * 8,
         out_specs=[VM] * 3,
         scratch_shapes=[
+            pltpu.VMEM((2, PER, LANES), F32),
             pltpu.VMEM((8, PER, LANES), F32),
             pltpu.VMEM((NTILE, PER, LANES), F32),
             pltpu.VMEM((8, PER, LANES), F32),
@@ -635,7 +660,7 @@
         ],
         compiler_params=pltpu.CompilerParams(collective_id=2, has_side_effects=True, vmem_limit_bytes=8 << 20),
         name="to_slots",
-    )(beta_one, hat_one, beta_two, hat_two, cells, home)
+    )(beta_one, hat_one, weight_sums, pull_sums, data, notes, cells, home)
     betas, hats, residual = pl.pallas_call(
         store_kernel,
         out_shape=[shape(2, NTILE * LANES), shape(2, NTILE * LANES), shape(NTILE, LANES)],

time: 66.1 us -> 58.8 us (0.89); the launches traced: 65.1 us -> 59.3 us
  Pallas kernels: 64.5 us -> 58.7 us
    pallas_call x3, Pallas kernels: 20.6 us -> 15.6 us  [the longest x1 6.42 us: body(): pl.pallas_call(halo_kernel, out_shape=[shape(80, LANES), shape(2, PER, LA...]
    pallas_call x1, Pallas kernels: 16.2 us -> 15.5 us  [body(): pl.pallas_call(return_kernel, out_shape=[shape(2, NTILE * LANES), shape(2...]
where the time goes in v3:
time: 58.8 us; the launch traced here: 59.3 us
  Pallas kernels  58.7 us (100%)
  between operations  0.67 us (1%)
    pallas_call x1, Pallas kernels, body(): pl.pallas_call(gather_kernel, out_shape=[shape(12, 40, LANES), shape(PER,...  26.8 us
    pallas_call x1, Pallas kernels, body(): pl.pallas_call(return_kernel, out_shape=[shape(2, NTILE * LANES), shape(2...  15.5 us
    pallas_call x1, Pallas kernels, body(): pl.pallas_call(halo_kernel, out_shape=[shape(80, LANES), shape(2, PER, LA...  6.42 us
    pallas_call x1, Pallas kernels, body(): pl.pallas_call(first_kernel, out_shape=sums, in_specs=[VM, VM, SM], out_s...  5.16 us
    pallas_call x1, Pallas kernels, body(): pl.pallas_call(second_kernel, out_shape=sums, in_specs=[VM] * 4 + [SM], o...  4.06 us

profile of v3, /device:TPU:1, one launch (start us, length us, event | category | flops | bytes accessed | tf_op | source)
XLA Modules:
  0.0 59.3 jit_solution(14877192236803647850)
XLA Ops:
  0.6 26.8 %to_owners.1 = (f32[12,40,128]{2,1,0:T(8,128)S(1)}, f32[16,128]{1,0:T(8,128)S(1)}, s32[2,32,128]{2,1,0:T(8,128)S(1)}, f32[8,128]{1,0:T(8,128)S(1)}, f32[6,16,128]{2,1,0:T(8,128)S(1)}) custom-call(f32[2,4096]{1,0:T(2,128)} %offsets_in.1, f32[2,4096]{1,0:T(2,128)} %design_in.1, f32[32,128]{1,0:T(8,128)} %bitcast.5, f32[32,128]{1,0:T(8,128)} %bitcast.6, ...), custom_call_target="tpu_custom_call" | custom-call | tf_op jit(solution)/shard_map/to_owners/pallas_call | solution.py:565
  27.5 5.2 %smooth_one.1 = (f32[16,256,128]{2,1,0:T(8,128)S(1)}, f32[16,256,128]{2,1,0:T(8,128)S(1)}) custom-call(f32[12,40,128]{2,1,0:T(8,128)S(1)} %get-tuple-element.24.data, f32[16,128]{1,0:T(8,128)S(1)} %get-tuple-element.25.notes, s32[2,32,128]{2,1,0:T(8,128)S(1)} %get-tuple-element.26.lists), custom_call_target="tpu_custom_call" | custom-call | tf_op jit(solution)/shard_map/smooth_one/pallas_call | solution.py:608
  32.6 6.4 %edges.1 = (f32[80,128]{1,0:T(8,128)S(1)}, f32[2,16,128]{2,1,0:T(8,128)S(1)}, f32[2,16,128]{2,1,0:T(8,128)S(1)}, f32[640,128]{1,0:T(8,128)S(1)}, f32[16,512,128]{2,1,0:T(8,128)S(1)}, /*index=5*/f32[16,128]{1,0:T(8,128)S(1)}) custom-call(f32[16,256,128]{2,1,0:T(8,128)S(1)} %get-tuple-element.27.weight_sums, f32[16,256,128]{2,1,0:T(8,128)S(1)} %get-tuple-element.28.pull_sums, ...), custom_call_target="tpu_custom_call" | custom-call | tf_op jit(solution)/shard_map/edges/pallas_call | solution.py:617
  39.1 4.1 %smooth_two.1 = (f32[16,256,128]{2,1,0:T(8,128)S(1)}, f32[16,256,128]{2,1,0:T(8,128)S(1)}) custom-call(f32[640,128]{1,0:T(8,128)S(1)} %get-tuple-element.31.cand, f32[80,128]{1,0:T(8,128)S(1)} %get-tuple-element.32.pull, f32[16,512,128]{2,1,0:T(8,128)S(1)} %get-tuple-element.33.fan, f32[16,128]{1,0:T(8,128)S(1)} %get-tuple-element.34.rates, ...), custom_call_target="tpu_custom_call" | custom-call | tf_op jit(solution)/shard_map/smooth_two/pallas_call | solution.py:637
  43.1 15.5 %to_slots.1 = (f32[2,4096]{1,0:T(2,128)S(1)}, f32[2,4096]{1,0:T(2,128)S(1)}, f32[32,128]{1,0:T(8,128)S(1)}) custom-call(f32[2,16,128]{2,1,0:T(8,128)S(1)} %get-tuple-element.29.beta_one, f32[2,16,128]{2,1,0:T(8,128)S(1)} %get-tuple-element.30.hat_one, f32[16,256,128]{2,1,0:T(8,128)S(1)} %get-tuple-element.35.weight_sums, ...), custom_call_target="tpu_custom_call" | custom-call | tf_op jit(solution)/shard_map/to_slots/pallas_call | solution.py:645
  58.7 0.7 %store.1 = (f32[2,4096]{1,0:T(2,128)}, f32[2,4096]{1,0:T(2,128)}, f32[32,128]{1,0:T(8,128)}) custom-call(f32[2,4096]{1,0:T(2,128)S(1)} %get-tuple-element.39.betas, f32[2,4096]{1,0:T(2,128)S(1)} %get-tuple-element.40.hats, f32[32,128]{1,0:T(8,128)S(1)} %get-tuple-element.41.residual), custom_call_target="tpu_custom_call" | custom-call | tf_op jit(solution)/shard_map/store/pallas_call | solution.py:664

commit v4 on v3

--- a/solution.py
+++ b/solution.py
@@ -49,6 +49,14 @@
 
 def signal(sem, region, tile):
     pl.semaphore_signal(sem, inc=1, device_id=(region, tile), device_id_type=pl.DeviceIdType.MESH)
+
+
+def links(k):
+    away = (0, 1, 2, 1)
+    return away[k // 2 % 4] + away[k // 8 % 4] + k % 2 / 2
+
+
+FAR_FIRST = sorted(range(1, NTILE), key=lambda k: -links(k))
 
 
 def each(low, high, step):
@@ -78,9 +86,11 @@
     down = lax.rem(region + NREGION - 1, NREGION)
 
     barrier = pltpu.get_barrier_semaphore()
-    each(1, NTILE, lambda o: signal(barrier, region, lax.rem(tile + o, NTILE)))
-    each(0, 16, lambda i: signal(barrier, up, group * 16 + i))
-    each(0, 16, lambda i: signal(barrier, down, group * 16 + i))
+    for k in range(15, -1, -1):
+        signal(barrier, up, jnp.bitwise_xor(tile, k))
+        signal(barrier, down, jnp.bitwise_xor(tile, k))
+    for k in FAR_FIRST:
+        signal(barrier, region, jnp.bitwise_xor(tile, k))
 
     loads = [
         pltpu.make_async_copy(source, place, load.at[k])
@@ -145,14 +155,15 @@
     pl.semaphore_wait(barrier, NTILE - 1 + 32)
 
     def to_middle(o):
-        other = lax.rem(tile + o, NTILE)
+        other = jnp.bitwise_xor(tile, o)
         held = jnp.minimum(lax.rem(other, 16), NPIECE - 1)
         return remote(
             stage.at[held, pl.ds(0, PER + 1)], rbuf.at[tile, pl.ds(0, PER + 1)],
             send1.at[o], recv1.at[tile], region, other,
         )
 
-    each(1, NTILE, lambda o: to_middle(o).start())
+    for k in FAR_FIRST:
+        to_middle(k).start()
     rbuf[tile] = stage[jnp.minimum(piece, NPIECE - 1)]
 
     number = lax.broadcasted_iota(jnp.int32, (640, LANES), 0)
@@ -170,7 +181,7 @@
     wanted[...] = jnp.where(allowed > 0, cell, -1).astype(F32)
 
     def from_source(o):
-        other = lax.rem(tile + o, NTILE)
+        other = jnp.bitwise_xor(tile, o)
         return remote(
             stage.at[0, pl.ds(0, PER + 1)], rbuf.at[other, pl.ds(0, PER + 1)],
             send1.at[o], recv1.at[other], region, other,
@@ -195,7 +206,7 @@
         msg[...] = moved.reshape(16, 40, LANES)
 
     def own_copy(o):
-        i = lax.rem(piece + o, 16)
+        i = jnp.bitwise_xor(piece, o)
         return remote(
             msg.at[i, pl.ds(0, 24)], recv.at[piece, pl.ds(0, 24)],
             send2.at[0, o], recv2.at[0, piece], region, group * 16 + i,
@@ -215,9 +226,12 @@
 
     @pl.when(piece < NPIECE)
     def _():
-        each(1, 16, lambda o: own_copy(o).start())
-        each(0, 16, lambda i: up_copy(i).start())
-        each(0, 16, lambda i: down_copy(i).start())
+        for k in sorted(range(16), key=lambda k: -links(k)):
+            up_copy(jnp.bitwise_xor(piece, k)).start()
+            down_copy(jnp.bitwise_xor(piece, k)).start()
+        for k in FAR_FIRST:
+            if k < 16:
+                own_copy(k).start()
         recv[piece, 0:24, :] = msg[piece, 0:24, :]
 
     def wait_own(p):
@@ -415,9 +429,15 @@
     return beta, jnp.where(live, cov * cov / total, 0.0)
 
 
+def edge_cells(a, b):
+    cols = range(4) if a == 0 else (0 if a == -1 else 3,)
+    rows = range(4) if b == 0 else (0 if b == -1 else 3,)
+    return [4 * r + c for r in rows for c in cols]
+
+
 def halo_kernel(
     weight_sums, pull_sums, data, notes, grid_out, beta_out, hat_out, cand_out, fan_out, rates_out,
-    own, totals, recv, send, land,
+    own, edge, totals, recv, send, land,
 ):
     region = lax.axis_index("region")
     tile = lax.axis_index("tile")
@@ -436,10 +456,15 @@
         beta_out[h] = beta
         hat_out[h] = hat
         own[h] = data[8 + h, 4:20, :] * (data[10 + h, 4:20, :] - data[4 + h, 4:20, :] * beta)
+    edge[...] = jnp.zeros((8, 8, LANES), F32)
+    for k, (a, b) in enumerate(steps):
+        for h in range(2):
+            for n, i in enumerate(edge_cells(a, b)):
+                edge[k, 4 * h + n : 4 * h + n + 1, :] = own[h, i : i + 1, :]
     pl.semaphore_wait(barrier, 8)
     copies = []
     for k, (a, b) in enumerate(steps):
-        copies.append(remote(own, recv.at[7 - k], send.at[k], land.at[7 - k], *place(a, b)))
+        copies.append(remote(edge.at[k], recv.at[7 - k], send.at[k], land.at[7 - k], *place(a, b)))
     for copy in copies:
         copy.start()
     prepare(1, data, notes, cand_out, fan_out, rates_out)
@@ -447,26 +472,22 @@
         copy.wait_recv()
     fits = {-1: region > 0, 0: None, 1: region < NREGION - 1}
     fits_row = {-1: owner > 0, 0: None, 1: owner < NTILE - 1}
-    at = {step: k for k, step in enumerate(steps)}
-
-    def take(h, a, b, low, high):
-        rows = recv[at[(a, b)], h, low:high, :]
-        for fit in (fits[a], fits_row[b]):
-            if fit is not None:
-                rows = jnp.where(fit, rows, 0.0)
-        return rows
-
     for h in range(2):
         to = 40 * h
         grid_out[to + 4 : to + 20, :] = own[h]
-        grid_out[to : to + 4, :] = take(h, 0, -1, 12, 16)
-        grid_out[to + 20 : to + 24, :] = take(h, 0, 1, 0, 4)
-        for a, edge, first in ((-1, 3, to + 24), (1, 0, to + 32)):
-            grid_out[first : first + 1, :] = take(h, a, -1, 12 + edge, 13 + edge)
-            for r in range(4):
-                grid_out[first + 1 + r : first + 2 + r, :] = take(h, a, 0, 4 * r + edge, 4 * r + edge + 1)
-            grid_out[first + 5 : first + 6, :] = take(h, a, 1, edge, edge + 1)
-            grid_out[first + 6 : first + 8, :] = jnp.zeros((2, LANES), F32)
+        for first in (to + 30, to + 38):
+            grid_out[first : first + 2, :] = jnp.zeros((2, LANES), F32)
+        for k, (a, b) in enumerate(steps):
+            many = len(edge_cells(-a, -b))
+            rows = recv[k, 4 * h : 4 * h + many, :]
+            for fit in (fits[a], fits_row[b]):
+                if fit is not None:
+                    rows = jnp.where(fit, rows, 0.0)
+            if a == 0:
+                first = to + (0 if b == -1 else 20)
+            else:
+                first = to + (24 if a == -1 else 32) + (0, 1, 5)[b + 1]
+            grid_out[first : first + many, :] = rows
     for copy in copies:
         copy.wait_send()
 
@@ -480,7 +501,8 @@
     group = tile // 8
     piece = lax.rem(tile, 8)
     barrier = pltpu.get_barrier_semaphore()
-    each(1, NTILE, lambda o: signal(barrier, region, lax.rem(tile + o, NTILE)))
+    for k in FAR_FIRST:
+        signal(barrier, region, jnp.bitwise_xor(tile, k))
     for h in range(2):
         stage[h] = beta_one[h]
         stage[2 + h] = hat_one[h]
@@ -488,12 +510,13 @@
     pl.semaphore_wait(barrier, NTILE - 1)
 
     def to_middle(o):
-        other = lax.rem(tile + o, NTILE)
+        other = jnp.bitwise_xor(tile, o)
         return remote(
             stage.at[lax.rem(other, 8)], rbuf.at[tile], send1.at[o], recv1.at[tile], region, other
         )
 
-    each(1, NTILE, lambda o: to_middle(o).start())
+    for k in FAR_FIRST:
+        to_middle(k).start()
     rbuf[tile] = stage[piece]
 
     row = cells[pl.ds(group, 1), :]
@@ -509,7 +532,7 @@
     hot = jnp.concatenate(hots, axis=1)
 
     def from_source(o):
-        other = lax.rem(tile + o, NTILE)
+        other = jnp.bitwise_xor(tile, o)
         return remote(stage.at[0], rbuf.at[other], send1.at[o], recv1.at[other], region, other)
 
     each(1, NTILE, lambda o: from_source(o).wait_recv())
@@ -517,16 +540,18 @@
     msg[...] = join3(jnp.dot(hot, spread, preferred_element_type=F32)).reshape(8, PER, LANES)
 
     def home_copy(o):
-        i = lax.rem(piece + o, 8)
+        i = jnp.bitwise_xor(piece, o)
         return remote(
             msg.at[i], recv.at[piece], send2.at[o], recv2.at[piece], region, group * 8 + i
         )
 
-    each(1, 8, lambda o: home_copy(o).start())
+    for k in FAR_FIRST:
+        if k < 8:
+            home_copy(k).start()
     recv[piece] = msg[piece]
 
     def from_middle(o):
-        p = lax.rem(piece + o, 8)
+        p = jnp.bitwise_xor(piece, o)
         return remote(msg.at[0], recv.at[p], send2.at[o], recv2.at[p], region, group * 8 + p)
 
     each(1, 8, lambda o: from_middle(o).wait_recv())
@@ -624,8 +649,9 @@
         out_specs=[VM] * 6,
         scratch_shapes=[
             pltpu.VMEM((2, PER, LANES), F32),
+            pltpu.VMEM((8, 8, LANES), F32),
             pltpu.VMEM((2, PER, LANES), F32),
-            pltpu.VMEM((8, 2, PER, LANES), F32),
+            pltpu.VMEM((8, 8, LANES), F32),
             DMA((8,)),
             DMA((8,)),
         ],

time: 58.8 us -> 56.8 us (0.966)
  Pallas kernels: 58.7 us -> 56.8 us
    pallas_call x1, Pallas kernels: 26.8 us -> 24.6 us  [body(): pl.pallas_call(gather_kernel, out_shape=[shape(12, 40, LANES), shape(PER,...]
    pallas_call x1, Pallas kernels: 6.42 us -> 7.58 us  [body(): pl.pallas_call(halo_kernel, out_shape=[shape(80, LANES), shape(2, PER, LA...]
    pallas_call x1, Pallas kernels: 5.16 us -> 4.52 us  [body(): pl.pallas_call(first_kernel, out_shape=sums, in_specs=[VM, VM, SM], out_s...]
where the time goes in v4:
time: 56.8 us; the launch traced here: 57.4 us
  Pallas kernels  56.8 us (100%)
  between operations  0.67 us (1%)
    pallas_call x1, Pallas kernels, body(): pl.pallas_call(gather_kernel, out_shape=[shape(12, 40, LANES), shape(PER,...  24.6 us
    pallas_call x1, Pallas kernels, body(): pl.pallas_call(return_kernel, out_shape=[shape(2, NTILE * LANES), shape(2...  15.5 us
    pallas_call x1, Pallas kernels, body(): pl.pallas_call(halo_kernel, out_shape=[shape(80, LANES), shape(2, PER, LA...  7.58 us
    pallas_call x1, Pallas kernels, body(): pl.pallas_call(first_kernel, out_shape=sums, in_specs=[VM, VM, SM], out_s...  4.52 us
    pallas_call x1, Pallas kernels, body(): pl.pallas_call(second_kernel, out_shape=sums, in_specs=[VM] * 4 + [SM], o...  3.88 us

profile of v4, /device:TPU:1, one launch (start us, length us, event | category | flops | bytes accessed | tf_op | source)
XLA Modules:
  0.0 57.4 jit_solution(11047351840208935218)
XLA Ops:
  0.6 24.6 %to_owners.1 = (f32[12,40,128]{2,1,0:T(8,128)S(1)}, f32[16,128]{1,0:T(8,128)S(1)}, s32[2,32,128]{2,1,0:T(8,128)S(1)}, f32[8,128]{1,0:T(8,128)S(1)}, f32[6,16,128]{2,1,0:T(8,128)S(1)}) custom-call(f32[2,4096]{1,0:T(2,128)} %offsets_in.1, f32[2,4096]{1,0:T(2,128)} %design_in.1, f32[32,128]{1,0:T(8,128)} %bitcast.5, f32[32,128]{1,0:T(8,128)} %bitcast.6, ...), custom_call_target="tpu_custom_call" | custom-call | tf_op jit(solution)/shard_map/to_owners/pallas_call | solution.py:590
  25.3 4.5 %smooth_one.1 = (f32[16,256,128]{2,1,0:T(8,128)S(1)}, f32[16,256,128]{2,1,0:T(8,128)S(1)}) custom-call(f32[12,40,128]{2,1,0:T(8,128)S(1)} %get-tuple-element.24.data, f32[16,128]{1,0:T(8,128)S(1)} %get-tuple-element.25.notes, s32[2,32,128]{2,1,0:T(8,128)S(1)} %get-tuple-element.26.lists), custom_call_target="tpu_custom_call" | custom-call | tf_op jit(solution)/shard_map/smooth_one/pallas_call | solution.py:633
  29.8 7.6 %edges.1 = (f32[80,128]{1,0:T(8,128)S(1)}, f32[2,16,128]{2,1,0:T(8,128)S(1)}, f32[2,16,128]{2,1,0:T(8,128)S(1)}, f32[640,128]{1,0:T(8,128)S(1)}, f32[16,512,128]{2,1,0:T(8,128)S(1)}, /*index=5*/f32[16,128]{1,0:T(8,128)S(1)}) custom-call(f32[16,256,128]{2,1,0:T(8,128)S(1)} %get-tuple-element.27.weight_sums, f32[16,256,128]{2,1,0:T(8,128)S(1)} %get-tuple-element.28.pull_sums, ...), custom_call_target="tpu_custom_call" | custom-call | tf_op jit(solution)/shard_map/edges/pallas_call | solution.py:642
  37.4 3.9 %smooth_two.1 = (f32[16,256,128]{2,1,0:T(8,128)S(1)}, f32[16,256,128]{2,1,0:T(8,128)S(1)}) custom-call(f32[640,128]{1,0:T(8,128)S(1)} %get-tuple-element.31.cand, f32[80,128]{1,0:T(8,128)S(1)} %get-tuple-element.32.pull, f32[16,512,128]{2,1,0:T(8,128)S(1)} %get-tuple-element.33.fan, f32[16,128]{1,0:T(8,128)S(1)} %get-tuple-element.34.rates, ...), custom_call_target="tpu_custom_call" | custom-call | tf_op jit(solution)/shard_map/smooth_two/pallas_call | solution.py:663
  41.3 15.5 %to_slots.1 = (f32[2,4096]{1,0:T(2,128)S(1)}, f32[2,4096]{1,0:T(2,128)S(1)}, f32[32,128]{1,0:T(8,128)S(1)}) custom-call(f32[2,16,128]{2,1,0:T(8,128)S(1)} %get-tuple-element.29.beta_one, f32[2,16,128]{2,1,0:T(8,128)S(1)} %get-tuple-element.30.hat_one, f32[16,256,128]{2,1,0:T(8,128)S(1)} %get-tuple-element.35.weight_sums, ...), custom_call_target="tpu_custom_call" | custom-call | tf_op jit(solution)/shard_map/to_slots/pallas_call | solution.py:671
  56.8 0.7 %store.1 = (f32[2,4096]{1,0:T(2,128)}, f32[2,4096]{1,0:T(2,128)}, f32[32,128]{1,0:T(8,128)}) custom-call(f32[2,4096]{1,0:T(2,128)S(1)} %get-tuple-element.39.betas, f32[2,4096]{1,0:T(2,128)S(1)} %get-tuple-element.40.hats, f32[32,128]{1,0:T(8,128)S(1)} %get-tuple-element.41.residual), custom_call_target="tpu_custom_call" | custom-call | tf_op jit(solution)/shard_map/store/pallas_call | solution.py:690

commit v5 on v4

--- a/solution.py
+++ b/solution.py
@@ -290,8 +290,8 @@
                     many = many + flag
             chunks = lax.shift_right_logical(filled[r].astype(jnp.int32) + CHUNK - 1, CHUNK.bit_length() - 1)
             value = jnp.where(lanes_f < many, todo, 240.0).astype(jnp.int32)
-            pairs = lax.shift_right_logical(many.astype(jnp.int32) + 1, 1)
-            value = jnp.where(lanes == 24, pairs, value)
+            groups = lax.shift_right_logical((many.astype(jnp.int32) + 2) * 11, 5)
+            value = jnp.where(lanes == 24, groups, value)
             value = jnp.where(lanes == 25, chunks, value)
             value = jnp.where(lanes == 26, filled[r].astype(jnp.int32), value)
             list_out[w, 8 * r - 8 : 8 * r, :] = value
@@ -312,7 +312,10 @@
 
 def prepare(which, data, notes, cand, fan, rates):
     rate = rate_of(which, notes)
-    rates[...] = -rate
+    rates[0:PER, :] = -rate
+    number = lax.broadcasted_iota(jnp.int32, (PER, LANES), 0)
+    rates[PER : 2 * PER, :] = (lax.bitwise_and(number, 3) + 1).astype(F32)
+    rates[2 * PER : 3 * PER, :] = (lax.shift_right_logical(number, 2) + 1).astype(F32)
     slot = lax.broadcasted_iota(jnp.int32, (40, LANES), 0)
     col = jnp.where(slot < 24, lax.rem(slot, 4) + 1, jnp.where(slot < 32, 0, 5)).astype(F32)
     row = jnp.where(
@@ -325,13 +328,19 @@
         cov = data[4 + 4 * which + h]
         for k, field in enumerate((x + col, y + row, cov * cov)):
             cand[pl.ds(320 * h + k, 40, stride=8), :] = field
-        for source in (2.0 * rate * x[4:20], 2.0 * rate * y[4:20]):
-            columns.append(jnp.transpose(jnp.concatenate(split3(source), axis=0)).astype(BF16))
+        along, upward = [
+            jnp.transpose(jnp.concatenate(split3(2.0 * rate * source), axis=0)).astype(BF16)
+            for source in (x[4:20], y[4:20])
+        ]
+        for low in range(0, LANES, CHUNK):
+            columns += [along[low : low + CHUNK], upward[low : low + CHUNK]]
     columns = jnp.concatenate(columns, axis=0)
     which_row = lax.bitwise_and(lax.broadcasted_iota(jnp.int32, (3 * PER, LANES), 0), PER - 1)
     for i in range(PER):
         pick = jnp.where(which_row == i, 1.0, 0.0).astype(BF16)
-        fan[i] = jnp.dot(columns, pick, preferred_element_type=F32)
+        fan[4 * LANES * i : 4 * LANES * (i + 1), :] = jnp.dot(
+            columns, pick, preferred_element_type=F32
+        )
 
 
 def sums_of(which, cand, pull, fan, rates, lists, weight_sums, pull_sums):
@@ -344,53 +353,61 @@
         total = total + lists[which, at, 24] * lists[which, at, 25]
 
     shape3 = (CHUNK // 8, 8, LANES)
+    spare = PER * 2 * LANES
 
     def row(ref, at):
         return jnp.broadcast_to(ref[pl.ds(at, 1), :], (8, LANES))
 
+    def rows(ref, at):
+        return ref[pl.ds(pl.multiple_of(at, CHUNK), CHUNK), :].reshape(shape3)
+
+    for ref in (weight_sums, pull_sums):
+        ref[spare : spare + CHUNK, :] = jnp.zeros((CHUNK, LANES), F32)
+
     def item(n, carry):
-        i, k, j, at, pairs, chunks, old_i, old_k, old_at, keep, powers, sums = carry
-        sums = [value * keep for value in sums]
-        for power, base in zip(powers, old_at):
+        i, k, j, out, at, groups, chunks, old_from, old_out, old_at, fars, powers = carry
+        x = [row(cand, base) - row(rates, PER + i) for base in at]
+        y = [row(cand, base + 1) - row(rates, 2 * PER + i) for base in at]
+        scale = row(rates, i)
+        u = rows(fan, 2 * out)
+        v = rows(fan, 2 * out + CHUNK)
+
+        weight_sum = rows(weight_sums, old_from)
+        pull_sum = rows(pull_sums, old_from)
+        for base, far, power in zip(old_at, fars, powers):
+            factor = jnp.exp2(far)
             weight = jnp.exp2(power)
-            sums[0] = sums[0] + weight * row(cand, base + 2)
-            sums[1] = sums[1] + weight * row(pull, lax.shift_right_logical(base, 3))
-        old = pl.ds(pl.multiple_of(old_k * CHUNK, CHUNK), CHUNK)
-        weight_sums[old_i, old, :] = sums[0].reshape(CHUNK, LANES)
-        pull_sums[old_i, old, :] = sums[1].reshape(CHUNK, LANES)
-
-        first = lax.shift_right_logical(k, 1) * 256 + lax.bitwise_and(k, 1) * CHUNK
-        u = fan[i, pl.ds(pl.multiple_of(first, CHUNK), CHUNK), :].reshape(shape3)
-        v = fan[i, pl.ds(pl.multiple_of(first + LANES, CHUNK), CHUNK), :].reshape(shape3)
-        scale = row(rates, i)
-        shift_x = (lax.bitwise_and(i, 3) + 1).astype(F32)
-        shift_y = (lax.shift_right_logical(i, 2) + 1).astype(F32)
-        powers = []
-        for base in at:
-            x = row(cand, base) - shift_x
-            y = row(cand, base + 1) - shift_y
-            powers.append(u * x + (v * y + (x * x + y * y) * scale))
-        keep = jnp.where(j == 0, 0.0, 1.0)
-        last = j + 1 == pairs
+            weight_sum = weight_sum + weight * (factor * row(cand, base + 2))
+            pull_sum = pull_sum + weight * (factor * row(pull, lax.shift_right_logical(base, 3)))
+        place = pl.ds(pl.multiple_of(old_out, CHUNK), CHUNK)
+        weight_sums[place, :] = weight_sum.reshape(CHUNK, LANES)
+        pull_sums[place, :] = pull_sum.reshape(CHUNK, LANES)
+
+        fars = tuple((x[g] * x[g] + y[g] * y[g]) * scale for g in range(3))
+        powers = tuple(u * x[g] + v * y[g] for g in range(3))
+        last = j + 1 == groups
         end = last & (k + 1 == chunks)
         next_j = jnp.where(last, 0, j + 1)
         next_k = jnp.where(end, 0, jnp.where(last, k + 1, k))
         next_i = jnp.minimum(jnp.where(end, i + 1, i), PER - 1)
+        next_out = next_i * (2 * LANES) + next_k * CHUNK
         here = line(next_i)
         return (
-            next_i, next_k, next_j,
-            (lists[which, here, 2 * next_j], lists[which, here, 2 * next_j + 1]),
-            lists[which, here, 24], lists[which, here, 25], i, k, at, keep, tuple(powers), tuple(sums),
-        )
-
-    zero = (fan[0, 0:CHUNK, :] * 0.0).reshape(shape3)
-    start = jnp.int32(0)
+            next_i, next_k, next_j, next_out,
+            tuple(lists[which, here, 3 * next_j + g] for g in range(3)),
+            lists[which, here, 24], lists[which, here, 25],
+            jnp.where(j == 0, spare, out), out, at, fars, powers,
+        )
+
+    zero = rows(fan, 0) * 0.0
+    none = row(rates, 0) * 0.0
+    begin = jnp.int32(0)
     lax.fori_loop(
         0, total + 1, item,
         (
-            start, start, start, (lists[which, 1, 0], lists[which, 1, 1]),
+            begin, begin, begin, begin, tuple(lists[which, 1, g] for g in range(3)),
             lists[which, 1, 24], lists[which, 1, 25],
-            start, start, (start, start), jnp.float32(0), (zero, zero), (zero, zero),
+            jnp.int32(spare), begin, (begin,) * 3, (none,) * 3, (zero,) * 3,
         ),
     )
 
@@ -410,7 +427,7 @@
     ones = jnp.ones((8, LANES), BF16)
     for k, ref in enumerate((weight_sums, pull_sums)):
         for i in range(PER):
-            values = ref[i, LANES * h : LANES * h + LANES, :]
+            values = ref[LANES * (2 * i + h) : LANES * (2 * i + h + 1), :]
             high = values.astype(BF16)
             low = (values - high.astype(F32)).astype(BF16)
             both = jnp.concatenate([high, low], axis=0)
@@ -628,8 +645,8 @@
             )
         )
     )
-    sums = [shape(PER, 2 * LANES, LANES)] * 2
-    tables = [(640, LANES), (80, LANES), (PER, 4 * LANES, LANES), (PER, LANES)]
+    sums = [shape((PER + 1) * 2 * LANES, LANES)] * 2
+    tables = [(640, LANES), (80, LANES), (PER * 4 * LANES, LANES), (3 * PER, LANES)]
     weight_sums, pull_sums = pl.pallas_call(
         first_kernel,
         out_shape=sums,
@@ -643,7 +660,7 @@
         halo_kernel,
         out_shape=[
             shape(80, LANES), shape(2, PER, LANES), shape(2, PER, LANES), shape(640, LANES),
-            shape(PER, 4 * LANES, LANES), shape(PER, LANES),
+            shape(PER * 4 * LANES, LANES), shape(3 * PER, LANES),
         ],
         in_specs=[VM] * 4,
         out_specs=[VM] * 6,

time: 56.8 us -> 55.7 us (0.981); the launches traced: 57.4 us -> 55.5 us
  Pallas kernels: 56.8 us -> 54.9 us
    pallas_call x1, Pallas kernels: 7.58 us -> 6.08 us  [body(): pl.pallas_call(halo_kernel, out_shape=[shape(80, LANES), shape(2, PER, LA...]
where the time goes in v5:
time: 55.7 us; the launch traced here: 55.5 us
  Pallas kernels  54.9 us (99%)
  between operations  0.67 us (1%)
    pallas_call x1, Pallas kernels, body(): pl.pallas_call(gather_kernel, out_shape=[shape(12, 40, LANES), shape(PER,...  24.7 us
    pallas_call x1, Pallas kernels, body(): pl.pallas_call(return_kernel, out_shape=[shape(2, NTILE * LANES), shape(2...  15.4 us
    pallas_call x1, Pallas kernels, body(): pl.pallas_call(halo_kernel, out_shape=[shape(80, LANES), shape(2, PER, LA...  6.08 us
    pallas_call x1, Pallas kernels, body(): pl.pallas_call(first_kernel, out_shape=sums, in_specs=[VM, VM, SM], out_s...  4.49 us
    pallas_call x1, Pallas kernels, body(): pl.pallas_call(second_kernel, out_shape=sums, in_specs=[VM] * 4 + [SM], o...  3.61 us

profile of v5, /device:TPU:1, one launch (start us, length us, event | category | flops | bytes accessed | tf_op | source)
XLA Modules:
  0.0 55.5 jit_solution(10675965290120423596)
XLA Ops:
  0.6 24.7 %to_owners.1 = (f32[12,40,128]{2,1,0:T(8,128)S(1)}, f32[16,128]{1,0:T(8,128)S(1)}, s32[2,32,128]{2,1,0:T(8,128)S(1)}, f32[8,128]{1,0:T(8,128)S(1)}, f32[6,16,128]{2,1,0:T(8,128)S(1)}) custom-call(f32[2,4096]{1,0:T(2,128)} %offsets_in.1, f32[2,4096]{1,0:T(2,128)} %design_in.1, f32[32,128]{1,0:T(8,128)} %bitcast.5, f32[32,128]{1,0:T(8,128)} %bitcast.6, ...), custom_call_target="tpu_custom_call" | custom-call | tf_op jit(solution)/shard_map/to_owners/pallas_call | solution.py:607
  25.3 4.5 %smooth_one.1 = (f32[4352,128]{1,0:T(8,128)S(1)}, f32[4352,128]{1,0:T(8,128)S(1)}) custom-call(f32[12,40,128]{2,1,0:T(8,128)S(1)} %get-tuple-element.24.data, f32[16,128]{1,0:T(8,128)S(1)} %get-tuple-element.25.notes, s32[2,32,128]{2,1,0:T(8,128)S(1)} %get-tuple-element.26.lists), custom_call_target="tpu_custom_call" | custom-call | tf_op jit(solution)/shard_map/smooth_one/pallas_call | solution.py:650
  29.8 6.1 %edges.1 = (f32[80,128]{1,0:T(8,128)S(1)}, f32[2,16,128]{2,1,0:T(8,128)S(1)}, f32[2,16,128]{2,1,0:T(8,128)S(1)}, f32[640,128]{1,0:T(8,128)S(1)}, f32[8192,128]{1,0:T(8,128)S(1)}, /*index=5*/f32[48,128]{1,0:T(8,128)S(1)}) custom-call(f32[4352,128]{1,0:T(8,128)S(1)} %get-tuple-element.27.weight_sums, f32[4352,128]{1,0:T(8,128)S(1)} %get-tuple-element.28.pull_sums, ...), custom_call_target="tpu_custom_call" | custom-call | tf_op jit(solution)/shard_map/edges/pallas_call | solution.py:659
  35.9 3.6 %smooth_two.1 = (f32[4352,128]{1,0:T(8,128)S(1)}, f32[4352,128]{1,0:T(8,128)S(1)}) custom-call(f32[640,128]{1,0:T(8,128)S(1)} %get-tuple-element.31.cand, f32[80,128]{1,0:T(8,128)S(1)} %get-tuple-element.32.pull, f32[8192,128]{1,0:T(8,128)S(1)} %get-tuple-element.33.fan, f32[48,128]{1,0:T(8,128)S(1)} %get-tuple-element.34.rates, ...), custom_call_target="tpu_custom_call" | custom-call | tf_op jit(solution)/shard_map/smooth_two/pallas_call | solution.py:680
  39.5 15.4 %to_slots.1 = (f32[2,4096]{1,0:T(2,128)S(1)}, f32[2,4096]{1,0:T(2,128)S(1)}, f32[32,128]{1,0:T(8,128)S(1)}) custom-call(f32[2,16,128]{2,1,0:T(8,128)S(1)} %get-tuple-element.29.beta_one, f32[2,16,128]{2,1,0:T(8,128)S(1)} %get-tuple-element.30.hat_one, f32[4352,128]{1,0:T(8,128)S(1)} %get-tuple-element.35.weight_sums, ...), custom_call_target="tpu_custom_call" | custom-call | tf_op jit(solution)/shard_map/to_slots/pallas_call | solution.py:688
  54.9 0.7 %store.1 = (f32[2,4096]{1,0:T(2,128)}, f32[2,4096]{1,0:T(2,128)}, f32[32,128]{1,0:T(8,128)}) custom-call(f32[2,4096]{1,0:T(2,128)S(1)} %get-tuple-element.39.betas, f32[2,4096]{1,0:T(2,128)S(1)} %get-tuple-element.40.hats, f32[32,128]{1,0:T(8,128)S(1)} %get-tuple-element.41.residual), custom_call_target="tpu_custom_call" | custom-call | tf_op jit(solution)/shard_map/store/pallas_call | solution.py:707

commit v6 on v5

--- a/solution.py
+++ b/solution.py
@@ -13,6 +13,7 @@
 PER = 16
 NPIECE = 13
 CHUNK = 64
+SHARE = (4, 1, 7, 3, 5, 0, 8)
 NREGION = 8
 NTILE = 32
 F32 = jnp.float32
@@ -266,14 +267,15 @@
         return jnp.broadcast_to(rows_of[8 * r : 8 * r + 8, at : at + 1], (8, LANES))
 
     lanes = lax.broadcasted_iota(jnp.int32, (8, LANES), 1)
-    lanes_f = lanes.astype(F32)
+    spots = lax.bitwise_and(lanes, 31)
+    spots_f = spots.astype(F32)
     over = lax.broadcasted_iota(jnp.int32, (8, LANES), 0)
     filled = [spread_lane(r, 0) for r in range(6)]
     near = [
         [filled[r] if a == 1 else pltpu.roll(filled[r], (1 - a) % 8, 0) for a in range(3)]
         for r in range(6)
     ]
-    for w in range(2):
+    for w, skipped, number in ((0, (), 0), (1, (), 1), (1, SHARE, 2)):
         for r in range(1, 5):
             many = jnp.zeros((8, LANES), F32)
             todo = jnp.zeros((8, LANES), F32)
@@ -284,17 +286,19 @@
                 c = over + (beside - 1)
                 t = jnp.where(c == 0, 24 + beyond, jnp.where(c == 5, 32 + beyond, beyond * 4 + c - 1))
                 at = (8 * t).astype(F32)
-                for h in range(2):
+                for h in range(1 if e in skipped else 0, 2):
                     flag = jnp.where(there > LANES * h, 1.0 if keep is None else keep, 0.0)
-                    todo = todo + jnp.where(many == lanes_f, flag * (at + 320.0 * h), 0.0)
+                    todo = todo + jnp.where(many == spots_f, flag * (at + 320.0 * h), 0.0)
                     many = many + flag
             chunks = lax.shift_right_logical(filled[r].astype(jnp.int32) + CHUNK - 1, CHUNK.bit_length() - 1)
-            value = jnp.where(lanes_f < many, todo, 240.0).astype(jnp.int32)
+            value = jnp.where(spots_f < many, todo, 240.0).astype(jnp.int32)
             groups = lax.shift_right_logical((many.astype(jnp.int32) + 2) * 11, 5)
-            value = jnp.where(lanes == 24, groups, value)
-            value = jnp.where(lanes == 25, chunks, value)
-            value = jnp.where(lanes == 26, filled[r].astype(jnp.int32), value)
-            list_out[w, 8 * r - 8 : 8 * r, :] = value
+            groups = jnp.maximum(groups, 1)
+            value = jnp.where(spots == 24, groups, value)
+            value = jnp.where(spots == 25, chunks, value)
+            value = jnp.where(spots == 26, filled[r].astype(jnp.int32), value)
+            band = value if r == 1 else jnp.where(lax.shift_right_logical(lanes, 5) == r - 1, value, band)
+        list_out[number] = band
 
     each(1, NTILE, lambda o: to_middle(o).wait_send())
 
@@ -344,13 +348,17 @@
 
 
 def sums_of(which, cand, pull, fan, rates, lists, weight_sums, pull_sums):
-    def line(i):
-        return lax.shift_right_logical(i, 2) * 8 + lax.bitwise_and(i, 3) + 1
+    def listed(kind, i, at):
+        band = lax.shift_right_logical(i, 2) * 32
+        return lists[kind, lax.bitwise_and(i, 3) + 1, band + at]
 
     total = jnp.int32(0)
     for i in range(PER):
-        at = 8 * (i // 4) + i % 4 + 1
-        total = total + lists[which, at, 24] * lists[which, at, 25]
+        r, at = i % 4 + 1, 32 * (i // 4) + 24
+        if which == 0:
+            total = total + lists[0, r, at] * lists[0, r, at + 1]
+        else:
+            total = total + lists[2, r, at] + lists[1, r, at] * (lists[1, r, at + 1] - 1)
 
     shape3 = (CHUNK // 8, 8, LANES)
     spare = PER * 2 * LANES
@@ -391,22 +399,23 @@
         next_k = jnp.where(end, 0, jnp.where(last, k + 1, k))
         next_i = jnp.minimum(jnp.where(end, i + 1, i), PER - 1)
         next_out = next_i * (2 * LANES) + next_k * CHUNK
-        here = line(next_i)
+        kind = 0 if which == 0 else jnp.where(next_k == 0, 2, 1)
         return (
             next_i, next_k, next_j, next_out,
-            tuple(lists[which, here, 3 * next_j + g] for g in range(3)),
-            lists[which, here, 24], lists[which, here, 25],
+            tuple(listed(kind, next_i, 3 * next_j + g) for g in range(3)),
+            listed(kind, next_i, 24), listed(kind, next_i, 25),
             jnp.where(j == 0, spare, out), out, at, fars, powers,
         )
 
     zero = rows(fan, 0) * 0.0
     none = row(rates, 0) * 0.0
     begin = jnp.int32(0)
+    kind = 2 * which
     lax.fori_loop(
         0, total + 1, item,
         (
-            begin, begin, begin, begin, tuple(lists[which, 1, g] for g in range(3)),
-            lists[which, 1, 24], lists[which, 1, 25],
+            begin, begin, begin, begin, tuple(lists[kind, 1, g] for g in range(3)),
+            lists[kind, 1, 24], lists[kind, 1, 25],
             jnp.int32(spare), begin, (begin,) * 3, (none,) * 3, (zero,) * 3,
         ),
     )
@@ -423,11 +432,15 @@
     sums_of(1, cand, pull, fan, rates, lists, weight_sums, pull_sums)
 
 
-def finish(which, h, data, notes, weight_sums, pull_sums, totals):
+def finish(which, h, data, notes, weight_sums, pull_sums, totals, more=None):
     ones = jnp.ones((8, LANES), BF16)
     for k, ref in enumerate((weight_sums, pull_sums)):
         for i in range(PER):
-            values = ref[LANES * (2 * i + h) : LANES * (2 * i + h + 1), :]
+            at = LANES * (2 * i + h)
+            values = ref[at : at + LANES, :]
+            if more is not None and h == 0:
+                added = values[:CHUNK] + more[k, CHUNK * i : CHUNK * (i + 1), :]
+                values = jnp.concatenate([added, values[CHUNK:]], axis=0)
             high = values.astype(BF16)
             low = (values - high.astype(F32)).astype(BF16)
             both = jnp.concatenate([high, low], axis=0)
@@ -450,6 +463,46 @@
     cols = range(4) if a == 0 else (0 if a == -1 else 3,)
     rows = range(4) if b == 0 else (0 if b == -1 else 3,)
     return [4 * r + c for r in rows for c in cols]
+
+
+def share(cand, pull, fan, rates, notes, keeps, more):
+    shape3 = (CHUNK // 8, 8, LANES)
+
+    def row(ref, at):
+        return jnp.broadcast_to(ref[pl.ds(at, 1), :], (8, LANES))
+
+    def rows(ref, at):
+        return ref[pl.ds(pl.multiple_of(at, CHUNK), CHUNK), :].reshape(shape3)
+
+    for e in SHARE:
+        kept = jnp.ones((PER, LANES), F32)
+        if e != 4:
+            kept = jnp.broadcast_to(notes[:, 12 + e : 13 + e], (PER, LANES))
+        keeps[PER * e : PER * (e + 1), :] = kept
+
+    def band(r):
+        for c in range(4):
+            i = 4 * r + c
+            u = rows(fan, 4 * LANES * i)
+            v = rows(fan, 4 * LANES * i + CHUNK)
+            scale = row(rates, i)
+            north = row(rates, 2 * PER + i)
+            weight_sum = jnp.zeros(shape3, F32)
+            pull_sum = jnp.zeros(shape3, F32)
+            for e in SHARE:
+                col, line = c + e // 3, r + e % 3
+                t = 24 + line if col == 0 else 32 + line if col == 5 else 4 * line + col - 1
+                x = row(cand, 8 * t) - (c + 1.0)
+                y = row(cand, 8 * t + 1) - north
+                factor = jnp.exp2((x * x + y * y) * scale) * row(keeps, PER * e + i)
+                weight = jnp.exp2(u * x + v * y)
+                weight_sum = weight_sum + weight * (factor * row(cand, 8 * t + 2))
+                pull_sum = pull_sum + weight * (factor * row(pull, t))
+            place = pl.ds(pl.multiple_of(CHUNK * i, CHUNK), CHUNK)
+            more[0, place, :] = weight_sum.reshape(CHUNK, LANES)
+            more[1, place, :] = pull_sum.reshape(CHUNK, LANES)
+
+    each(0, 4, band)
 
 
 def halo_kernel(
@@ -510,8 +563,8 @@
 
 
 def return_kernel(
-    beta_one, hat_one, weight_sums, pull_sums, data, notes, cells, home, betas, hats, residual,
-    totals, stage, rbuf, msg, recv, send1, recv1, send2, recv2,
+    beta_one, hat_one, weight_sums, pull_sums, data, notes, cells, home, cand, pull, fan, rates,
+    betas, hats, residual, keeps, more, totals, stage, rbuf, msg, recv, send1, recv1, send2, recv2,
 ):
     region = lax.axis_index("region")
     tile = lax.axis_index("tile")
@@ -520,10 +573,13 @@
     barrier = pltpu.get_barrier_semaphore()
     for k in FAR_FIRST:
         signal(barrier, region, jnp.bitwise_xor(tile, k))
+    share(cand, pull, fan, rates, notes, keeps, more)
     for h in range(2):
         stage[h] = beta_one[h]
         stage[2 + h] = hat_one[h]
-        stage[4 + h], stage[6 + h] = finish(1, h, data, notes, weight_sums, pull_sums, totals)
+        stage[4 + h], stage[6 + h] = finish(
+            1, h, data, notes, weight_sums, pull_sums, totals, more
+        )
     pl.semaphore_wait(barrier, NTILE - 1)
 
     def to_middle(o):
@@ -607,7 +663,7 @@
     data, notes, lists, cells, home = pl.pallas_call(
         gather_kernel,
         out_shape=[
-            shape(12, 40, LANES), shape(PER, LANES), shape(2, 32, LANES, dtype=jnp.int32),
+            shape(12, 40, LANES), shape(PER, LANES), shape(3, 8, LANES, dtype=jnp.int32),
             shape(8, LANES), shape(6, PER, LANES),
         ],
         in_specs=[HB] * 8,
@@ -688,9 +744,11 @@
     betas, hats, residual = pl.pallas_call(
         return_kernel,
         out_shape=[shape(2, NTILE * LANES), shape(2, NTILE * LANES), shape(NTILE, LANES)],
-        in_specs=[VM] * 8,
+        in_specs=[VM] * 12,
         out_specs=[VM] * 3,
         scratch_shapes=[
+            pltpu.VMEM((9 * PER, LANES), F32),
+            pltpu.VMEM((2, PER * CHUNK, LANES), F32),
             pltpu.VMEM((2, PER, LANES), F32),
             pltpu.VMEM((8, PER, LANES), F32),
             pltpu.VMEM((NTILE, PER, LANES), F32),
@@ -701,9 +759,9 @@
             DMA((8,)),
             DMA((8,)),
         ],
-        compiler_params=pltpu.CompilerParams(collective_id=2, has_side_effects=True, vmem_limit_bytes=8 << 20),
+        compiler_params=pltpu.CompilerParams(collective_id=2, has_side_effects=True, vmem_limit_bytes=16 << 20),
         name="to_slots",
-    )(beta_one, hat_one, weight_sums, pull_sums, data, notes, cells, home)
+    )(beta_one, hat_one, weight_sums, pull_sums, data, notes, cells, home, cand, grid, fan, rates)
     betas, hats, residual = pl.pallas_call(
         store_kernel,
         out_shape=[shape(2, NTILE * LANES), shape(2, NTILE * LANES), shape(NTILE, LANES)],

time: 55.7 us -> 54.3 us (0.975)
  Pallas kernels: 54.9 us -> 53.5 us
    pallas_call x1, Pallas kernels: 3.61 us -> 2.29 us  [body(): pl.pallas_call(second_kernel, out_shape=sums, in_specs=[VM] * 4 + [SM], o...]
where the time goes in v6:
time: 54.3 us; the launch traced here: 54.2 us
  Pallas kernels  53.5 us (99%)
  between operations  0.67 us (1%)
    pallas_call x1, Pallas kernels, body(): pl.pallas_call(gather_kernel, out_shape=[shape(12, 40, LANES), shape(PER,...  24.7 us
    pallas_call x1, Pallas kernels, body(): pl.pallas_call(return_kernel, out_shape=[shape(2, NTILE * LANES), shape(2...  15.5 us
    pallas_call x1, Pallas kernels, body(): pl.pallas_call(halo_kernel, out_shape=[shape(80, LANES), shape(2, PER, LA...  6.31 us
    pallas_call x1, Pallas kernels, body(): pl.pallas_call(first_kernel, out_shape=sums, in_specs=[VM, VM, SM], out_s...  4.08 us
    pallas_call x1, Pallas kernels, body(): pl.pallas_call(second_kernel, out_shape=sums, in_specs=[VM] * 4 + [SM], o...  2.29 us

profile of v6, /device:TPU:1, one launch (start us, length us, event | category | flops | bytes accessed | tf_op | source)
XLA Modules:
  0.0 54.2 jit_solution(9346195038935541765)
XLA Ops:
  0.6 24.7 %to_owners.1 = (f32[12,40,128]{2,1,0:T(8,128)S(1)}, f32[16,128]{1,0:T(8,128)S(1)}, s32[3,8,128]{2,1,0:T(8,128)S(1)}, f32[8,128]{1,0:T(8,128)S(1)}, f32[6,16,128]{2,1,0:T(8,128)S(1)}) custom-call(f32[2,4096]{1,0:T(2,128)} %offsets_in.1, f32[2,4096]{1,0:T(2,128)} %design_in.1, f32[32,128]{1,0:T(8,128)} %bitcast.5, f32[32,128]{1,0:T(8,128)} %bitcast.6, ...), custom_call_target="tpu_custom_call" | custom-call | tf_op jit(solution)/shard_map/to_owners/pallas_call | solution.py:663
  25.3 4.1 %smooth_one.1 = (f32[4352,128]{1,0:T(8,128)S(1)}, f32[4352,128]{1,0:T(8,128)S(1)}) custom-call(f32[12,40,128]{2,1,0:T(8,128)S(1)} %get-tuple-element.24.data, f32[16,128]{1,0:T(8,128)S(1)} %get-tuple-element.25.notes, s32[3,8,128]{2,1,0:T(8,128)S(1)} %get-tuple-element.26.lists), custom_call_target="tpu_custom_call" | custom-call | tf_op jit(solution)/shard_map/smooth_one/pallas_call | solution.py:706
  29.4 6.3 %edges.1 = (f32[80,128]{1,0:T(8,128)S(1)}, f32[2,16,128]{2,1,0:T(8,128)S(1)}, f32[2,16,128]{2,1,0:T(8,128)S(1)}, f32[640,128]{1,0:T(8,128)S(1)}, f32[8192,128]{1,0:T(8,128)S(1)}, /*index=5*/f32[48,128]{1,0:T(8,128)S(1)}) custom-call(f32[4352,128]{1,0:T(8,128)S(1)} %get-tuple-element.27.weight_sums, f32[4352,128]{1,0:T(8,128)S(1)} %get-tuple-element.28.pull_sums, ...), custom_call_target="tpu_custom_call" | custom-call | tf_op jit(solution)/shard_map/edges/pallas_call | solution.py:715
  35.8 2.3 %smooth_two.1 = (f32[4352,128]{1,0:T(8,128)S(1)}, f32[4352,128]{1,0:T(8,128)S(1)}) custom-call(f32[640,128]{1,0:T(8,128)S(1)} %get-tuple-element.31.cand, f32[80,128]{1,0:T(8,128)S(1)} %get-tuple-element.32.pull, f32[8192,128]{1,0:T(8,128)S(1)} %get-tuple-element.33.fan, f32[48,128]{1,0:T(8,128)S(1)} %get-tuple-element.34.rates, ...), custom_call_target="tpu_custom_call" | custom-call | tf_op jit(solution)/shard_map/smooth_two/pallas_call | solution.py:736
  38.0 15.5 %to_slots.1 = (f32[2,4096]{1,0:T(2,128)S(1)}, f32[2,4096]{1,0:T(2,128)S(1)}, f32[32,128]{1,0:T(8,128)S(1)}) custom-call(f32[2,16,128]{2,1,0:T(8,128)S(1)} %get-tuple-element.29.beta_one, f32[2,16,128]{2,1,0:T(8,128)S(1)} %get-tuple-element.30.hat_one, f32[4352,128]{1,0:T(8,128)S(1)} %get-tuple-element.35.weight_sums, ...), custom_call_target="tpu_custom_call" | custom-call | tf_op jit(solution)/shard_map/to_slots/pallas_call | solution.py:744
  53.5 0.7 %store.1 = (f32[2,4096]{1,0:T(2,128)}, f32[2,4096]{1,0:T(2,128)}, f32[32,128]{1,0:T(8,128)}) custom-call(f32[2,4096]{1,0:T(2,128)S(1)} %get-tuple-element.39.betas, f32[2,4096]{1,0:T(2,128)S(1)} %get-tuple-element.40.hats, f32[32,128]{1,0:T(8,128)S(1)} %get-tuple-element.41.residual), custom_call_target="tpu_custom_call" | custom-call | tf_op jit(solution)/shard_map/store/pallas_call | solution.py:765

commit v7 on v6

--- a/solution.py
+++ b/solution.py
@@ -75,7 +75,7 @@
 
 def gather_kernel(
     offsets_in, design_in, target_in, prior_in, counts_in, width_in, reach_in, cells_in,
-    data_out, width_out, list_out, cells_out, home_out,
+    data_out, width_out, list_one, list_two, cells_out, home_out,
     offs, design, target, prior, counts, widths, reach, cells, notes, rows_of,
     wanted, stage, rbuf, msg, recv, load, send1, recv1, send2, recv2,
 ):
@@ -253,10 +253,8 @@
             send2.at[2, 0], recv2.at[2, p], up, group * 16 + p,
         ).wait_recv()
 
-    each(0, NPIECE, wait_own)
-    each(0, NPIECE, wait_sides)
-    for p in range(12):
-        data_out[p] = recv[p]
+    wait_own(12)
+    wait_sides(12)
     width_out[...] = recv[12, 4:20, :]
     for r in range(6):
         rows_of[8 * r : 8 * r + 1, :] = recv[12, 24 + r : 25 + r, :]
@@ -275,7 +273,7 @@
         [filled[r] if a == 1 else pltpu.roll(filled[r], (1 - a) % 8, 0) for a in range(3)]
         for r in range(6)
     ]
-    for w, skipped, number in ((0, (), 0), (1, (), 1), (1, SHARE, 2)):
+    for w, skipped, place in ((0, (), list_one.at[0]), (1, (), list_two.at[0]), (1, SHARE, list_two.at[1])):
         for r in range(1, 5):
             many = jnp.zeros((8, LANES), F32)
             todo = jnp.zeros((8, LANES), F32)
@@ -298,7 +296,11 @@
             value = jnp.where(spots == 25, chunks, value)
             value = jnp.where(spots == 26, filled[r].astype(jnp.int32), value)
             band = value if r == 1 else jnp.where(lax.shift_right_logical(lanes, 5) == r - 1, value, band)
-        list_out[number] = band
+        place[...] = band
+    each(0, NPIECE - 1, wait_own)
+    each(0, NPIECE - 1, wait_sides)
+    for p in range(12):
+        data_out[p] = recv[p]
 
     each(1, NTILE, lambda o: to_middle(o).wait_send())
 
@@ -358,7 +360,7 @@
         if which == 0:
             total = total + lists[0, r, at] * lists[0, r, at + 1]
         else:
-            total = total + lists[2, r, at] + lists[1, r, at] * (lists[1, r, at + 1] - 1)
+            total = total + lists[1, r, at] + lists[0, r, at] * (lists[0, r, at + 1] - 1)
 
     shape3 = (CHUNK // 8, 8, LANES)
     spare = PER * 2 * LANES
@@ -399,7 +401,7 @@
         next_k = jnp.where(end, 0, jnp.where(last, k + 1, k))
         next_i = jnp.minimum(jnp.where(end, i + 1, i), PER - 1)
         next_out = next_i * (2 * LANES) + next_k * CHUNK
-        kind = 0 if which == 0 else jnp.where(next_k == 0, 2, 1)
+        kind = 0 if which == 0 else jnp.where(next_k == 0, 1, 0)
         return (
             next_i, next_k, next_j, next_out,
             tuple(listed(kind, next_i, 3 * next_j + g) for g in range(3)),
@@ -410,7 +412,7 @@
     zero = rows(fan, 0) * 0.0
     none = row(rates, 0) * 0.0
     begin = jnp.int32(0)
-    kind = 2 * which
+    kind = which
     lax.fori_loop(
         0, total + 1, item,
         (
@@ -660,14 +662,14 @@
 
 
 def body(offsets, design, target, beta_second, counts, kernel_width, reach, assignment):
-    data, notes, lists, cells, home = pl.pallas_call(
+    data, notes, list_one, list_two, cells, home = pl.pallas_call(
         gather_kernel,
         out_shape=[
-            shape(12, 40, LANES), shape(PER, LANES), shape(3, 8, LANES, dtype=jnp.int32),
-            shape(8, LANES), shape(6, PER, LANES),
+            shape(12, 40, LANES), shape(PER, LANES), shape(1, 8, LANES, dtype=jnp.int32),
+            shape(2, 8, LANES, dtype=jnp.int32), shape(8, LANES), shape(6, PER, LANES),
         ],
         in_specs=[HB] * 8,
-        out_specs=[VM] * 5,
+        out_specs=[VM] * 6,
         scratch_shapes=[
             pltpu.VMEM((2, NTILE * LANES), F32),
             pltpu.VMEM((2, NTILE * LANES), F32),
@@ -711,7 +713,7 @@
         scratch_shapes=[pltpu.VMEM(dims, F32) for dims in tables],
         compiler_params=pltpu.CompilerParams(vmem_limit_bytes=16 << 20),
         name="smooth_one",
-    )(data, notes, lists)
+    )(data, notes, list_one)
     grid, beta_one, hat_one, cand, fan, rates = pl.pallas_call(
         halo_kernel,
         out_shape=[
@@ -740,7 +742,7 @@
         out_specs=[VM] * 2,
         compiler_params=pltpu.CompilerParams(vmem_limit_bytes=16 << 20),
         name="smooth_two",
-    )(cand, grid, fan, rates, lists)
+    )(cand, grid, fan, rates, list_two)
     betas, hats, residual = pl.pallas_call(
         return_kernel,
         out_shape=[shape(2, NTILE * LANES), shape(2, NTILE * LANES), shape(NTILE, LANES)],

time: 54.3 us -> 54.2 us (level); the launches traced: 54.2 us -> 54.7 us
  Pallas kernels: 53.5 us -> 54.1 us
    pallas_call x1, Pallas kernels: 15.5 us -> 16.6 us  [body(): pl.pallas_call(return_kernel, out_shape=[shape(2, NTILE * LANES), shape(2...]
    pallas_call x1, Pallas kernels: 6.31 us -> 7.3 us  [body(): pl.pallas_call(halo_kernel, out_shape=[shape(80, LANES), shape(2, PER, LA...]
    pallas_call x1, Pallas kernels: 4.08 us -> 3.31 us  [body(): pl.pallas_call(first_kernel, out_shape=sums, in_specs=[VM, VM, SM], out_s...]
where the time goes in v7:
time: 54.2 us; the launch traced here: 54.7 us
  Pallas kernels  54.1 us (100%)
  between operations  0.67 us (1%)
    pallas_call x1, Pallas kernels, body(): pl.pallas_call(gather_kernel, out_shape=[shape(12, 40, LANES), shape(PER,...  24.4 us
    pallas_call x1, Pallas kernels, body(): pl.pallas_call(return_kernel, out_shape=[shape(2, NTILE * LANES), shape(2...  16.6 us
    pallas_call x1, Pallas kernels, body(): pl.pallas_call(halo_kernel, out_shape=[shape(80, LANES), shape(2, PER, LA...  7.3 us
    pallas_call x1, Pallas kernels, body(): pl.pallas_call(first_kernel, out_shape=sums, in_specs=[VM, VM, SM], out_s...  3.31 us
    pallas_call x1, Pallas kernels, body(): pl.pallas_call(second_kernel, out_shape=sums, in_specs=[VM] * 4 + [SM], o...  1.76 us

profile of v7, /device:TPU:1, one launch (start us, length us, event | category | flops | bytes accessed | tf_op | source)
XLA Modules:
  0.0 54.7 jit_solution(18444798953073629454)
XLA Ops:
  0.6 24.4 %to_owners.1 = (f32[12,40,128]{2,1,0:T(8,128)S(1)}, f32[16,128]{1,0:T(8,128)S(1)}, s32[1,8,128]{2,1,0:T(8,128)S(1)}, s32[2,8,128]{2,1,0:T(8,128)S(1)}, f32[8,128]{1,0:T(8,128)S(1)}, /*index=5*/f32[6,16,128]{2,1,0:T(8,128)S(1)}) custom-call(f32[2,4096]{1,0:T(2,128)} %offsets_in.1, f32[2,4096]{1,0:T(2,128)} %design_in.1, f32[32,128]{1,0:T(8,128)} %bitcast.5, ...), custom_call_target="tpu_custom_call" | custom-call | tf_op jit(solution)/shard_map/to_owners/pallas_call | solution.py:665
  25.1 3.3 %smooth_one.1 = (f32[4352,128]{1,0:T(8,128)S(1)}, f32[4352,128]{1,0:T(8,128)S(1)}) custom-call(f32[12,40,128]{2,1,0:T(8,128)S(1)} %get-tuple-element.25.data, f32[16,128]{1,0:T(8,128)S(1)} %get-tuple-element.26.notes, s32[1,8,128]{2,1,0:T(8,128)S(1)} %get-tuple-element.27.lists), custom_call_target="tpu_custom_call" | custom-call | tf_op jit(solution)/shard_map/smooth_one/pallas_call | solution.py:708
  28.4 7.3 %edges.1 = (f32[80,128]{1,0:T(8,128)S(1)}, f32[2,16,128]{2,1,0:T(8,128)S(1)}, f32[2,16,128]{2,1,0:T(8,128)S(1)}, f32[640,128]{1,0:T(8,128)S(1)}, f32[8192,128]{1,0:T(8,128)S(1)}, /*index=5*/f32[48,128]{1,0:T(8,128)S(1)}) custom-call(f32[4352,128]{1,0:T(8,128)S(1)} %get-tuple-element.28.weight_sums, f32[4352,128]{1,0:T(8,128)S(1)} %get-tuple-element.29.pull_sums, ...), custom_call_target="tpu_custom_call" | custom-call | tf_op jit(solution)/shard_map/edges/pallas_call | solution.py:717
  35.7 1.8 %smooth_two.1 = (f32[4352,128]{1,0:T(8,128)S(1)}, f32[4352,128]{1,0:T(8,128)S(1)}) custom-call(f32[640,128]{1,0:T(8,128)S(1)} %get-tuple-element.32.cand, f32[80,128]{1,0:T(8,128)S(1)} %get-tuple-element.33.pull, f32[8192,128]{1,0:T(8,128)S(1)} %get-tuple-element.34.fan, f32[48,128]{1,0:T(8,128)S(1)} %get-tuple-element.35.rates, ...), custom_call_target="tpu_custom_call" | custom-call | tf_op jit(solution)/shard_map/smooth_two/pallas_call | solution.py:738
  37.5 16.6 %to_slots.1 = (f32[2,4096]{1,0:T(2,128)S(1)}, f32[2,4096]{1,0:T(2,128)S(1)}, f32[32,128]{1,0:T(8,128)S(1)}) custom-call(f32[2,16,128]{2,1,0:T(8,128)S(1)} %get-tuple-element.30.beta_one, f32[2,16,128]{2,1,0:T(8,128)S(1)} %get-tuple-element.31.hat_one, f32[4352,128]{1,0:T(8,128)S(1)} %get-tuple-element.37.weight_sums, ...), custom_call_target="tpu_custom_call" | custom-call | tf_op jit(solution)/shard_map/to_slots/pallas_call | solution.py:746
  54.1 0.7 %store.1 = (f32[2,4096]{1,0:T(2,128)}, f32[2,4096]{1,0:T(2,128)}, f32[32,128]{1,0:T(8,128)}) custom-call(f32[2,4096]{1,0:T(2,128)S(1)} %get-tuple-element.41.betas, f32[2,4096]{1,0:T(2,128)S(1)} %get-tuple-element.42.hats, f32[32,128]{1,0:T(8,128)S(1)} %get-tuple-element.43.residual), custom_call_target="tpu_custom_call" | custom-call | tf_op jit(solution)/shard_map/store/pallas_call | solution.py:767

commit v8 on v7

--- a/solution.py
+++ b/solution.py
@@ -13,7 +13,7 @@
 PER = 16
 NPIECE = 13
 CHUNK = 64
-SHARE = (4, 1, 7, 3, 5, 0, 8)
+SHARE = (4, 1, 7, 3, 5, 0, 8, 2, 6)
 NREGION = 8
 NTILE = 32
 F32 = jnp.float32

time: 54.2 us -> 53.6 us (0.989); the launches traced: 54.7 us -> 53 us
  Pallas kernels: 54.1 us -> 52.3 us
    pallas_call x1, Pallas kernels: 16.6 us -> 14.1 us  [body(): pl.pallas_call(return_kernel, out_shape=[shape(2, NTILE * LANES), shape(2...]
    pallas_call x1, Pallas kernels: 7.3 us -> 5.39 us  [body(): pl.pallas_call(halo_kernel, out_shape=[shape(80, LANES), shape(2, PER, LA...]
    pallas_call x1, Pallas kernels: 3.31 us -> 4.78 us  [body(): pl.pallas_call(first_kernel, out_shape=sums, in_specs=[VM, VM, SM], out_s...]
    pallas_call x1, Pallas kernels: 1.76 us -> 2.95 us  [body(): pl.pallas_call(second_kernel, out_shape=sums, in_specs=[VM] * 4 + [SM], o...]
where the time goes in v8:
time: 53.6 us; the launch traced here: 53 us
  Pallas kernels  52.3 us (98%)
  between operations  0.67 us (1%)
    pallas_call x1, Pallas kernels, body(): pl.pallas_call(gather_kernel, out_shape=[shape(12, 40, LANES), shape(PER,...  24.4 us
    pallas_call x1, Pallas kernels, body(): pl.pallas_call(return_kernel, out_shape=[shape(2, NTILE * LANES), shape(2...  14.1 us
    pallas_call x1, Pallas kernels, body(): pl.pallas_call(halo_kernel, out_shape=[shape(80, LANES), shape(2, PER, LA...  5.39 us
    pallas_call x1, Pallas kernels, body(): pl.pallas_call(first_kernel, out_shape=sums, in_specs=[VM, VM, SM], out_s...  4.78 us
    pallas_call x1, Pallas kernels, body(): pl.pallas_call(second_kernel, out_shape=sums, in_specs=[VM] * 4 + [SM], o...  2.95 us

profile of v8, /device:TPU:1, one launch (start us, length us, event | category | flops | bytes accessed | tf_op | source)
XLA Modules:
  0.0 53.0 jit_solution(5924478362012653693)
XLA Ops:
  0.6 24.4 %to_owners.1 = (f32[12,40,128]{2,1,0:T(8,128)S(1)}, f32[16,128]{1,0:T(8,128)S(1)}, s32[1,8,128]{2,1,0:T(8,128)S(1)}, s32[2,8,128]{2,1,0:T(8,128)S(1)}, f32[8,128]{1,0:T(8,128)S(1)}, /*index=5*/f32[6,16,128]{2,1,0:T(8,128)S(1)}) custom-call(f32[2,4096]{1,0:T(2,128)} %offsets_in.1, f32[2,4096]{1,0:T(2,128)} %design_in.1, f32[32,128]{1,0:T(8,128)} %bitcast.5, ...), custom_call_target="tpu_custom_call" | custom-call | tf_op jit(solution)/shard_map/to_owners/pallas_call | solution.py:665
  25.1 4.8 %smooth_one.1 = (f32[4352,128]{1,0:T(8,128)S(1)}, f32[4352,128]{1,0:T(8,128)S(1)}) custom-call(f32[12,40,128]{2,1,0:T(8,128)S(1)} %get-tuple-element.25.data, f32[16,128]{1,0:T(8,128)S(1)} %get-tuple-element.26.notes, s32[1,8,128]{2,1,0:T(8,128)S(1)} %get-tuple-element.27.lists), custom_call_target="tpu_custom_call" | custom-call | tf_op jit(solution)/shard_map/smooth_one/pallas_call | solution.py:708
  29.9 5.4 %edges.1 = (f32[80,128]{1,0:T(8,128)S(1)}, f32[2,16,128]{2,1,0:T(8,128)S(1)}, f32[2,16,128]{2,1,0:T(8,128)S(1)}, f32[640,128]{1,0:T(8,128)S(1)}, f32[8192,128]{1,0:T(8,128)S(1)}, /*index=5*/f32[48,128]{1,0:T(8,128)S(1)}) custom-call(f32[4352,128]{1,0:T(8,128)S(1)} %get-tuple-element.28.weight_sums, f32[4352,128]{1,0:T(8,128)S(1)} %get-tuple-element.29.pull_sums, ...), custom_call_target="tpu_custom_call" | custom-call | tf_op jit(solution)/shard_map/edges/pallas_call | solution.py:717
  35.3 2.9 %smooth_two.1 = (f32[4352,128]{1,0:T(8,128)S(1)}, f32[4352,128]{1,0:T(8,128)S(1)}) custom-call(f32[640,128]{1,0:T(8,128)S(1)} %get-tuple-element.32.cand, f32[80,128]{1,0:T(8,128)S(1)} %get-tuple-element.33.pull, f32[8192,128]{1,0:T(8,128)S(1)} %get-tuple-element.34.fan, f32[48,128]{1,0:T(8,128)S(1)} %get-tuple-element.35.rates, ...), custom_call_target="tpu_custom_call" | custom-call | tf_op jit(solution)/shard_map/smooth_two/pallas_call | solution.py:738
  38.2 14.1 %to_slots.1 = (f32[2,4096]{1,0:T(2,128)S(1)}, f32[2,4096]{1,0:T(2,128)S(1)}, f32[32,128]{1,0:T(8,128)S(1)}) custom-call(f32[2,16,128]{2,1,0:T(8,128)S(1)} %get-tuple-element.30.beta_one, f32[2,16,128]{2,1,0:T(8,128)S(1)} %get-tuple-element.31.hat_one, f32[4352,128]{1,0:T(8,128)S(1)} %get-tuple-element.37.weight_sums, ...), custom_call_target="tpu_custom_call" | custom-call | tf_op jit(solution)/shard_map/to_slots/pallas_call | solution.py:746
  52.3 0.7 %store.1 = (f32[2,4096]{1,0:T(2,128)}, f32[2,4096]{1,0:T(2,128)}, f32[32,128]{1,0:T(8,128)}) custom-call(f32[2,4096]{1,0:T(2,128)S(1)} %get-tuple-element.41.betas, f32[2,4096]{1,0:T(2,128)S(1)} %get-tuple-element.42.hats, f32[32,128]{1,0:T(8,128)S(1)} %get-tuple-element.43.residual), custom_call_target="tpu_custom_call" | custom-call | tf_op jit(solution)/shard_map/store/pallas_call | solution.py:767
